TPU v7x, 512 devices: a whole 4x8x8 slice. The times are simulated.
512 devices in a mesh: dom: 32 (over x, z), slab: 16 (over y, core).
Axes of the slice: x: 4, y: 8, z: 8, core: 2. Of those that a mesh axis runs over, the one named last changes fastest.
Arguments:
- equivariant_embedding: bfloat16 [32, 16, 128, 25, 128], P('dom', 'slab'), may hold values from -6 to 6
- cartesian_coordinates: float32 [32, 16, 3, 128], P('dom', 'slab'), may hold values from 0 to 40
- element_identity: int32 [32, 16, 128], P('dom', 'slab'), may hold values from 0 to 3
- occupied_site_totals: int32 [32, 16], P('dom', 'slab'), may hold values from 32 to 128, as said below
- halo_export_indices: int32 [32, 16, 32], P('dom', 'slab'), may hold values from 0 to 127, as said below
- adjacency_rows: int32 [32, 16, 128, 64], P('dom', 'slab'), may hold values from -1 to 415, as said below
- attention_source_weights: bfloat16 [128, 128], replicated, may hold values from -0.5 to 0.5
- attention_target_weights: bfloat16 [128, 128], replicated, may hold values from -0.5 to 0.5
- degree_channel_mixer: bfloat16 [5, 128, 128], replicated, may hold values from -0.5 to 0.5
- affinity_output_head: float32 [5, 128], replicated, may hold values from -0.25 to 0.25
- baseline_affinity_per_element: float32 [4], replicated, may hold values from -3 to 3
- chemical_stiffness: float32 [4], replicated, may hold values from 2 to 5
- reciprocal_lattice_points: float32 [3, 4096], replicated, may hold values from -1 to 1
- ewald_weighting: float32 [4096], replicated, may hold values from 0.005 to 0.05
Outputs:
- charges: float32 [32, 16, 128], P('dom', 'slab')
- forces: float32 [32, 16, 3, 128], P('dom', 'slab')
Inputs may be any that keep to these rules, and one draw needn't show every extreme that they name: `occupied_site_totals`: live atoms occupy the slots below a device's count; the count of at least one device is 128. `halo_export_indices`: every entry is a live slot of its own device, below that device's occupied_site_totals. `adjacency_rows`: entries -1 are empty; an atom's filled entries come first, are distinct, name live own slots or ghost rows, never the middle block (3a+b = 4); slots that are not live have only -1; every live atom has at least 16 filled entries and some atom of every device has 64.
All inputs are finite; a program needn't handle non-finite values.
Results may differ from a plain program's by a relative error of at most 0.0021.
Values may be sent and summed in bfloat16 or wider, within the bound.
A program may use at most 64 MiB of HBM per device.

v0:
```python
import math

import jax
import jax.numpy as jnp
from jax import lax
from jax.sharding import PartitionSpec as P

ITERS = 4


highest_accuracy_mode = lax.Precision.HIGHEST


def extended(cells, sides, width):
    for axis, dim in sides:
        count = lax.axis_size(axis)
        head = lax.slice_in_dim(cells, 0, width, axis=dim)
        tail = lax.slice_in_dim(cells, cells.shape[dim] - width, cells.shape[dim], axis=dim)
        cells = jnp.concatenate(
            [
                lax.ppermute(tail, axis, [(i, (i + 1) % count) for i in range(count)]),
                cells,
                lax.ppermute(head, axis, [((i + 1) % count, i) for i in range(count)]),
            ],
            axis=dim,
        )
    return cells


def project_values(row_block, degree_channel_mixer):
    pieces = []
    for degree in range(degree_channel_mixer.shape[0]):
        first_comp = degree * degree
        last_comp = (degree + 1) * (degree + 1)
        product_part = jnp.einsum(
            "ncd,de->nce",
            row_block[:, first_comp:last_comp, :],
            degree_channel_mixer[degree],
            preferred_element_type=jnp.float32,
        )
        pieces.append(product_part.astype(jnp.bfloat16))
    joined = jnp.concatenate(pieces, axis=1)
    return joined.reshape(row_block.shape[0], -1)


def readout_sum(message, affinity_output_head):
    result_sum = jnp.sum(message[:, 0, :] * affinity_output_head[0], axis=1)
    for degree in range(1, affinity_output_head.shape[0]):
        first_comp = degree * degree
        last_comp = (degree + 1) * (degree + 1)
        part_sq = message[:, first_comp:last_comp, :] * message[:, first_comp:last_comp, :]
        channel_norm = jnp.sqrt(jnp.sum(part_sq, axis=1) + 1e-06)
        result_sum = result_sum + jnp.sum(channel_norm * affinity_output_head[degree], axis=1)
    return result_sum


def reciprocal_angles(shard_layout, reciprocal_lattice_points):
    initial_addend = shard_layout[0][:, None] * reciprocal_lattice_points[0][None, :]
    central_addend = shard_layout[1][:, None] * reciprocal_lattice_points[1][None, :]
    final_addend = shard_layout[2][:, None] * reciprocal_lattice_points[2][None, :]
    return initial_addend + central_addend + final_addend


def norm_of(vector_in):
    return lax.psum(jnp.sum(vector_in * vector_in), ("dom", "slab"))


def shards(
    equivariant_embedding,
    cartesian_coordinates,
    element_identity,
    occupied_site_totals,
    halo_export_indices,
    adjacency_rows,
    attention_source_weights,
    attention_target_weights,
    degree_channel_mixer,
    affinity_output_head,
    baseline_affinity_per_element,
    chemical_stiffness,
    reciprocal_lattice_points,
    ewald_weighting,
):
    atom_slots = equivariant_embedding.shape[2]
    channels = equivariant_embedding.shape[4]
    own_feats = equivariant_embedding[0, 0]
    scalar_ch = own_feats[:, 0, :]
    queries = jnp.dot(
        scalar_ch, attention_source_weights, preferred_element_type=jnp.float32
    ).astype(jnp.bfloat16)
    own_keys = jnp.dot(
        scalar_ch, attention_target_weights, preferred_element_type=jnp.float32
    ).astype(jnp.bfloat16)
    own_values = project_values(own_feats, degree_channel_mixer)
    packed = jnp.concatenate([own_keys, own_values], axis=1)
    outgoing = packed[halo_export_indices[0, 0]]
    arrived = extended(outgoing[None, None], (("dom", 0), ("slab", 1)), 1)
    arrived = arrived.reshape(-1, packed.shape[1])
    table_keys = jnp.concatenate([own_keys, arrived[:, :channels]], axis=0)
    table_values = jnp.concatenate([own_values, arrived[:, channels:]], axis=0)
    table_size = table_keys.shape[0]
    neigh_dev = adjacency_rows[0, 0]
    row_ids = jnp.broadcast_to(jnp.arange(atom_slots, dtype=jnp.int32)[:, None], neigh_dev.shape)
    col_ids = jnp.where(neigh_dev >= 0, neigh_dev, table_size)
    neighbour_mask = (
        jnp.zeros((atom_slots, table_size), jnp.float32).at[row_ids, col_ids].set(1.0, mode="drop")
    )
    scores = jnp.einsum("ac,tc->at", queries, table_keys, preferred_element_type=jnp.float32)
    weights = jnp.where(
        neighbour_mask > 0.0, jax.nn.sigmoid(scores / math.sqrt(channels)) * 0.125, 0.0
    ).astype(jnp.bfloat16)
    message = jnp.dot(weights, table_values, preferred_element_type=jnp.float32).reshape(
        atom_slots, -1, channels
    )
    element_hit = (
        element_identity[0, 0][:, None]
        == jnp.arange(baseline_affinity_per_element.shape[0], dtype=jnp.int32)[None, :]
    ).astype(jnp.float32)
    electroneg = readout_sum(message, affinity_output_head) + jnp.sum(
        element_hit * baseline_affinity_per_element[None, :], axis=1
    )
    hard_diag = jnp.sum(element_hit * chemical_stiffness[None, :], axis=1)
    live_slots = jnp.arange(atom_slots, dtype=jnp.int32) < occupied_site_totals[0, 0]
    rhs_vec = jnp.where(live_slots, -electroneg, 0.0)
    angle_table_fetch = reciprocal_angles(cartesian_coordinates[0, 0], reciprocal_lattice_points)
    even_harmonic_entries = jnp.cos(angle_table_fetch)
    odd_harmonic_entries = jnp.sin(angle_table_fetch)
    recip_scale = 1.0 / math.sqrt(lax.axis_size("dom") * lax.axis_size("slab") * atom_slots)

    def local_factors(vector_in):
        return (
            jnp.dot(vector_in, even_harmonic_entries, precision=highest_accuracy_mode),
            jnp.dot(vector_in, odd_harmonic_entries, precision=highest_accuracy_mode),
        )

    charges = jnp.zeros_like(rhs_vec)
    residual = rhs_vec
    structure_factor_real = jnp.zeros_like(ewald_weighting)
    structure_factor_imag = jnp.zeros_like(ewald_weighting)
    direction = rhs_vec
    resid_norm = norm_of(residual)
    for iteration in range(ITERS):
        dir_cos, dir_sin = local_factors(direction)
        cos_sum, sin_sum = lax.psum((dir_cos, dir_sin), ("dom", "slab"))
        recip_part = jnp.dot(
            even_harmonic_entries, ewald_weighting * cos_sum, precision=highest_accuracy_mode
        ) + jnp.dot(
            odd_harmonic_entries, ewald_weighting * sin_sum, precision=highest_accuracy_mode
        )
        image_vec = jnp.where(live_slots, hard_diag * direction + recip_scale * recip_part, 0.0)
        step_size = resid_norm / lax.psum(jnp.sum(direction * image_vec), ("dom", "slab"))
        charges = charges + step_size * direction
        residual = residual - step_size * image_vec
        structure_factor_real = structure_factor_real + step_size * cos_sum
        structure_factor_imag = structure_factor_imag + step_size * sin_sum
        norm_next = norm_of(residual)
        direction = residual + norm_next / resid_norm * direction
        resid_norm = norm_next
    own_cos, own_sin = local_factors(charges)
    structure_factor_real, structure_factor_imag = lax.psum((own_cos, own_sin), ("dom", "slab"))
    odd_part_result = jnp.dot(
        odd_harmonic_entries,
        (ewald_weighting * structure_factor_real)[:, None] * reciprocal_lattice_points.T,
        precision=highest_accuracy_mode,
    )
    even_part_result = jnp.dot(
        even_harmonic_entries,
        (ewald_weighting * structure_factor_imag)[:, None] * reciprocal_lattice_points.T,
        precision=highest_accuracy_mode,
    )
    efield_rows = recip_scale * (odd_part_result - even_part_result)
    forces = (charges[:, None] * efield_rows).T
    return (charges.reshape(1, 1, atom_slots), forces.reshape(1, 1, 3, atom_slots))


def solution(mesh):
    placed = (
        P("dom", "slab", None, None, None),
        P("dom", "slab", None, None),
        P("dom", "slab", None),
        P("dom", "slab"),
        P("dom", "slab", None),
        P("dom", "slab", None, None),
        P(),
        P(),
        P(),
        P(),
        P(),
        P(),
        P(),
        P(),
    )
    return jax.shard_map(
        shards,
        mesh=mesh,
        in_specs=placed,
        out_specs=(P("dom", "slab", None), P("dom", "slab", None, None)),
        check_vma=False,
    )
```

profile of v0, /device:TPU:1, one launch (start us, length us, event | category | flops | bytes accessed | tf_op | source)
XLA Modules:
  0.0 1409.6 jit_solution(3128413423806610155)
XLA Ops:
  0.7 1.0 fusion.58
  1.7 1.1 fusion.56
  2.8 1.2 fusion.48
  4.0 1.2 fusion.47
  5.2 1.3 fusion.46
  6.5 0.8 copy.45
  7.3 0.9 convolution_convert_fusion.5
  8.4 0.7 gather_fusion
  9.1 4.8 collective-permute-start
  14.0 10.8 collective-permute-start.1
  24.9 0.1 and_reduce_fusion
  25.0 0.1 copy.40
  25.2 0.9 convolution_convert_fusion.6
  26.7 30.7 %scatter_custom_fusion = f32[53248]{0:T(1024)S(1)} fusion(s32[8192]{0:T(1024)S(1)} %reshape.124, f32[8192]{0:T(1024)S(1)} %broadcast.111, f32[]{:T(128)} %constant.9.clone.1), kind=kCustom, calls=%fused_computation.216 | custom fusion | bytes 212996
  57.5 0.1 select_reduce_fusion
  57.7 2.1 collective-permute-start.2
  59.9 7.3 collective-permute-done.2
  67.2 2.5 collective-permute-done.3
  69.7 0.2 pad_maximum_fusion
  69.9 0.1 slice.124
  70.0 2.6 fusion
  72.7 1.1 fusion.267
  73.7 1.0 fusion.268
  74.7 1.1 fusion.263
  75.8 0.9 fusion.271
  76.8 0.1 multiply_reduce_fusion.4
  76.9 1.0 fusion.286
  77.8 0.1 multiply_reduce_fusion.2
  78.0 8.1 fusion.24
  86.1 8.4 fusion.44
  94.5 97.3 %all-reduce.5 = (f32[4096]{0:T(1024)S(1)}, f32[4096]{0:T(1024)S(1)}) all-reduce(f32[4096]{0:T(1024)S(1)} %bitcast.228, f32[4096]{0:T(1024)S(1)} %bitcast.227), channel_id=1, replica_groups=mesh['dom'=32,'slab'=16] {'dom','slab'}, use_global_device_ids=true, to_apply=%region_15.16 | all-reduce | flops 8192 | bytes 65536 | tf_op jit(solution)/shard_map/psum | solution.py:144
  191.7 8.7 fusion.68
  200.4 9.5 multiply_reduce_fusion.10
  210.0 94.7 %all-reduce.4 = (f32[]{:T(128)}, f32[]{:T(128)}) all-reduce(f32[]{:T(128)} %get-tuple-element.11, f32[]{:T(128)} %get-tuple-element.10), channel_id=1, replica_groups=mesh['dom'=32,'slab'=16] {'dom','slab'}, use_global_device_ids=true, to_apply=%region_12.13 | all-reduce | flops 2 | bytes 16 | tf_op jit(solution)/shard_map/psum | solution.py:65
  306.0 0.6 multiply_reduce_fusion.9
  306.6 96.1 %psum.130 = f32[]{:T(128)} all-reduce(f32[]{:T(128)} %get-tuple-element.30), channel_id=1, replica_groups=mesh['dom'=32,'slab'=16] {'dom','slab'}, use_global_device_ids=true, to_apply=%region_19.20 | all-reduce | flops 1 | bytes 8 | tf_op jit(solution)/shard_map/psum | solution.py:65
  403.9 8.1 fusion.20
  412.0 8.3 fusion.40
  420.3 95.1 %all-reduce.3 = (f32[4096]{0:T(1024)S(1)}, f32[4096]{0:T(1024)S(1)}) all-reduce(f32[4096]{0:T(1024)S(1)} %bitcast.230, f32[4096]{0:T(1024)S(1)} %bitcast.229), channel_id=1, replica_groups=mesh['dom'=32,'slab'=16] {'dom','slab'}, use_global_device_ids=true, to_apply=%region_21.22 | all-reduce | flops 8192 | bytes 65536 | tf_op jit(solution)/shard_map/psum | solution.py:144
  515.4 8.7 fusion.71
  524.1 9.8 multiply_reduce_fusion.8
  533.9 95.1 %psum.133 = f32[]{:T(128)} all-reduce(f32[]{:T(128)} %get-tuple-element.54), channel_id=1, replica_groups=mesh['dom'=32,'slab'=16] {'dom','slab'}, use_global_device_ids=true, to_apply=%region_23.24 | all-reduce | flops 1 | bytes 8 | tf_op jit(solution)/shard_map/psum | solution.py:151
  630.2 0.7 multiply_reduce_fusion.7
  630.9 96.1 %psum.134 = f32[]{:T(128)} all-reduce(f32[]{:T(128)} %get-tuple-element.28), channel_id=1, replica_groups=mesh['dom'=32,'slab'=16] {'dom','slab'}, use_global_device_ids=true, to_apply=%region_25.26 | all-reduce | flops 1 | bytes 8 | tf_op jit(solution)/shard_map/psum | solution.py:65
  728.2 8.1 fusion.16
  736.3 8.6 fusion.36
  744.9 94.9 %all-reduce.2 = (f32[4096]{0:T(1024)S(1)}, f32[4096]{0:T(1024)S(1)}) all-reduce(f32[4096]{0:T(1024)S(1)} %bitcast.232, f32[4096]{0:T(1024)S(1)} %bitcast.231), channel_id=1, replica_groups=mesh['dom'=32,'slab'=16] {'dom','slab'}, use_global_device_ids=true, to_apply=%region_27.28 | all-reduce | flops 8192 | bytes 65536 | tf_op jit(solution)/shard_map/psum | solution.py:144
  839.9 8.7 fusion.74
  848.6 9.4 multiply_reduce_fusion.6
  858.0 95.7 %psum.137 = f32[]{:T(128)} all-reduce(f32[]{:T(128)} %get-tuple-element.56), channel_id=1, replica_groups=mesh['dom'=32,'slab'=16] {'dom','slab'}, use_global_device_ids=true, to_apply=%region_29.30 | all-reduce | flops 1 | bytes 8 | tf_op jit(solution)/shard_map/psum | solution.py:151
  954.9 0.6 multiply_reduce_fusion.5
  955.5 95.7 %psum.138 = f32[]{:T(128)} all-reduce(f32[]{:T(128)} %multiply_reduce_fusion.5), channel_id=1, replica_groups=mesh['dom'=32,'slab'=16] {'dom','slab'}, use_global_device_ids=true, to_apply=%region_31.32 | all-reduce | flops 1 | bytes 8 | tf_op jit(solution)/shard_map/psum | solution.py:65
  1052.5 8.1 fusion.12
  1060.6 8.3 fusion.32
  1068.9 95.5 %all-reduce.1 = (f32[4096]{0:T(1024)S(1)}, f32[4096]{0:T(1024)S(1)}) all-reduce(f32[4096]{0:T(1024)S(1)} %bitcast.234, f32[4096]{0:T(1024)S(1)} %bitcast.233), channel_id=1, replica_groups=mesh['dom'=32,'slab'=16] {'dom','slab'}, use_global_device_ids=true, to_apply=%region_33.34 | all-reduce | flops 8192 | bytes 65536 | tf_op jit(solution)/shard_map/psum | solution.py:144
  1164.5 8.7 fusion.77
  1173.2 9.8 fusion.264
  1182.9 94.9 %psum.141 = f32[]{:T(128)} all-reduce(f32[]{:T(128)} %fusion.264), channel_id=1, replica_groups=mesh['dom'=32,'slab'=16] {'dom','slab'}, use_global_device_ids=true, to_apply=%region_35.36 | all-reduce | flops 1 | bytes 8 | tf_op jit(solution)/shard_map/psum | solution.py:151
  1279.2 8.1 fusion.8
  1287.3 8.3 fusion.26
  1295.6 95.9 %all-reduce = (f32[4096]{0:T(1024)S(1)}, f32[4096]{0:T(1024)S(1)}) all-reduce(f32[4096]{0:T(1024)S(1)} %bitcast.236, f32[4096]{0:T(1024)S(1)} %bitcast.235), channel_id=1, replica_groups=mesh['dom'=32,'slab'=16] {'dom','slab'}, use_global_device_ids=true, to_apply=%region_37.38 | all-reduce | flops 8192 | bytes 65536 | tf_op jit(solution)/shard_map/psum | solution.py:160
  1391.6 8.4 fusion.6
  1400.0 8.8 fusion.65
  1408.8 0.6 copy.48
  (55 shorter events, 0.6 us)
Async XLA Ops:
  0.6 6.7 copy-start
  0.6 7.6 copy-start.13
  7.3 17.4 %copy-start.4 = (s32[1,1,128,64]{2,3,1,0:T(8,128)S(1)}, s32[1,1,128,64]{2,3,1,0:T(8,128)}, u32[]{:S(2)}) copy-start(s32[1,1,128,64]{2,3,1,0:T(8,128)} %param.19) | copy-start | bytes 98308
  7.3 17.5 %copy-start.7 = (s32[2]{0:T(128)S(1)}, s32[2]{0:T(128)}, u32[]{:S(2)}) copy-start(s32[2]{0:T(128)} %constant.34) | copy-start | bytes 28
  8.3 16.6 %copy-start.8 = (s32[2]{0:T(128)S(1)}, s32[2]{0:T(128)}, u32[]{:S(2)}) copy-start(s32[2]{0:T(128)} %constant.37) | copy-start | bytes 28
  8.3 16.9 %copy-start.3 = (bf16[128,128]{1,0:T(8,128)(2,1)S(1)}, bf16[128,128]{1,0:T(8,128)(2,1)}, u32[]{:S(2)}) copy-start(bf16[128,128]{1,0:T(8,128)(2,1)} %param.20) | copy-start | bytes 98308
  8.3 17.8 %copy-start.5 = (f32[5,128]{1,0:T(8,128)S(1)}, f32[5,128]{1,0:T(8,128)}, u32[]{:S(2)}) copy-start(f32[5,128]{1,0:T(8,128)} %param.23) | copy-start | bytes 7684
  8.3 49.1 %copy-start.9 = (f32[4]{0:T(128)S(1)}, f32[4]{0:T(128)}, u32[]{:S(2)}) copy-start(f32[4]{0:T(128)} %param.25) | copy-start | bytes 52
  8.3 49.1 %copy-start.10 = (s32[1,1,128]{2,1,0:T(1,128)S(1)}, s32[1,1,128]{2,1,0:T(1,128)}, u32[]{:S(2)}) copy-start(s32[1,1,128]{2,1,0:T(1,128)} %param.16) | copy-start | bytes 1540
  8.3 49.1 %copy-start.11 = (f32[4]{0:T(128)S(1)}, f32[4]{0:T(128)}, u32[]{:S(2)}) copy-start(f32[4]{0:T(128)} %param.24) | copy-start | bytes 52
  8.4 49.2 %copy-start.6 = (f32[1,1,3,128]{3,1,2,0:T(1,128)S(1)}, f32[1,1,3,128]{3,1,2,0:T(1,128)}, u32[]{:S(2)}) copy-start(f32[1,1,3,128]{3,1,2,0:T(1,128)} %param.15) | copy-start | bytes 4612
  8.4 51.4 %copy-start.2 = (f32[3,4096]{1,0:T(4,128)S(1)}, f32[3,4096]{1,0:T(4,128)}, u32[]{:S(2)}) copy-start(f32[3,4096]{1,0:T(4,128)} %param.26) | copy-start | bytes 147460
  9.1 48.4 %collective-permute-start = (bf16[1,1,32,3328]{3,2,1,0:T(8,128)(2,1)S(1)}, bf16[1,1,32,3328]{3,2,1,0:T(8,128)(2,1)S(1)}, u32[]{:S(2)}, u32[]{:S(2)}) collective-permute-start(bf16[1,1,32,3328]{3,2,1,0:T(8,128)(2,1)S(1)} %bitcast.206), channel_id=1, source_target_pairs={{0,16},{16,32},{32,48},{48,64},{64,80},{80,96},{96,112},{112,128},... | collective-permute-start | bytes 638984 | tf_op jit(solution)/shard_map/ppermute | solution.py:21
  14.0 43.6 %collective-permute-start.1 = (bf16[1,1,32,3328]{3,2,1,0:T(8,128)(2,1)S(1)}, bf16[1,1,32,3328]{3,2,1,0:T(8,128)(2,1)S(1)}, u32[]{:S(2)}, u32[]{:S(2)}) collective-permute-start(bf16[1,1,32,3328]{3,2,1,0:T(8,128)(2,1)S(1)} %bitcast.207), channel_id=1, source_target_pairs={{16,0},{32,16},{48,32},{64,48},{80,64},{96,80},{112,96},{128,112},... | collective-permute-start | bytes 638984 | tf_op jit(solution)/shard_map/ppermute | solution.py:23
  57.7 9.5 collective-permute-start.2
  59.8 9.8 collective-permute-start.3
  86.1 105.6 %copy-start.1 = (f32[4096]{0:T(1024)S(1)}, f32[4096]{0:T(1024)}, u32[]{:S(2)}) copy-start(f32[4096]{0:T(1024)} %param.27) | copy-start | bytes 49156
  1279.1 16.5 %copy-start.12 = (f32[128]{0:T(128)}, f32[128]{0:T(128)S(1)}, u32[]{:S(2)}) copy-start(f32[128]{0:T(128)S(1)} %get-tuple-element.27) | copy-start | bytes 1540
where the time goes:
time: 1410 us
  blocking collectives  1150 us (82%)
  matrix products  183 us (13%)
  local copies, waits for them, and re-layouts  33.2 us (2%)
  starting transfers between devices  17.8 us (1%)
    psum x4, blocking collectives, shards(): cos_sum, sin_sum = lax.psum((dir_cos, dir_sin), ('dom', 'slab'))  383 us
    psum x4, blocking collectives, norm_of(): return lax.psum(jnp.sum(vector_in * vector_in), ('dom', 'slab'))  383 us
    psum x3, blocking collectives, shards(): lax.psum(jnp.sum(direction * image_vec), ('dom', 'slab'))  286 us
    psum x1, blocking collectives, shards(): lax.psum((own_cos, own_sin), ('dom', 'slab'))  95.9 us
    dot_general x5, matrix products, local_factors(): jnp.dot(vector_in, odd_harmonic_entries, precision=highest_accuracy_mode)  42 us
    dot_general x5, matrix products, local_factors(): jnp.dot(vector_in, even_harmonic_entries, precision=highest_accuracy_mode)  40.5 us
    dot_general x4, matrix products, shards(): jnp.dot(even_harmonic_entries, ewald_weighting * cos_sum, precision=highe...  38.5 us
    dot_general x4, matrix products, shards(): jnp.dot(odd_harmonic_entries, ewald_weighting * sin_sum, precision=highes...  34.8 us
  transfers between devices with their start and end apart: 4, of which 2 were waited for; matrix products, arithmetic and copies ran while one was open for 2% of the time, Pallas kernels for 0%

commit v1 on v0

v1 whole, which is shorter than its diff:
```python
import math

import jax
import jax.numpy as jnp
from jax import lax
from jax.experimental import pallas as pl
from jax.experimental.pallas import tpu as pltpu
from jax.sharding import PartitionSpec as P

ITERS = 4
CHIPS_X = 4
LANES = 128
MESH = pl.DeviceIdType.MESH
F32 = jnp.float32

HALF_PI_PARTS = (1.5703125, 4.837512969970703125e-4, 7.54978995489188216e-8)


def sine_cosine(phase):
    quadrant = jnp.round(phase * (2.0 / math.pi))
    reduced = phase - quadrant * HALF_PI_PARTS[0]
    reduced = reduced - quadrant * HALF_PI_PARTS[1]
    reduced = reduced - quadrant * HALF_PI_PARTS[2]
    square = reduced * reduced
    odd = (-1.9515295891e-4 * square + 8.3321608736e-3) * square - 1.6666654611e-1
    odd = odd * square * reduced + reduced
    even = (2.443315711809948e-5 * square - 1.388731625493765e-3) * square
    even = (even + 4.166664568298827e-2) * square * square - 0.5 * square + 1.0
    turn = quadrant.astype(jnp.int32)
    swap = (turn & 1) == 1
    sine = jnp.where(swap, even, odd)
    cosine = jnp.where(swap, odd, even)
    sine = jnp.where((turn & 2) == 2, -sine, sine)
    cosine = jnp.where(((turn + 1) & 2) == 2, -cosine, cosine)
    return sine, cosine


def lines(shape):
    chips_x, chips_y, chips_z = shape
    dom, slab = lax.axis_index("dom"), lax.axis_index("slab")
    x, z = dom // chips_z, dom % chips_z
    y, core = slab // 2, slab % 2

    def place(px, py, pz, pc):
        return (px * chips_z + pz, py * 2 + pc)

    ring = chips_y
    along = [
        place(x, (y + j * (1 - core)) % chips_y, (z + j * core) % chips_z, core)
        for j in range(1, ring)
    ]
    across = [
        place(x, (y + j * core) % chips_y, (z + j * (1 - core)) % chips_z, core)
        for j in range(1, ring)
    ]
    pair = place(x, y, z, 1 - core)
    last = [
        place((x + i // 2) % chips_x, y, z, (core + i % 2) % 2) for i in range(1, 2 * chips_x)
    ]
    return core, pair, along, across, last


def row_of(column, eye):
    return jnp.sum(jnp.where(eye, column, 0.0), axis=0, keepdims=True)


def column_of(row, eye):
    wide = jnp.broadcast_to(row, (LANES, LANES))
    return jnp.broadcast_to(
        jnp.sum(jnp.where(eye, wide, 0.0), axis=1, keepdims=True), (LANES, LANES)
    )


def identity_mask():
    return lax.broadcasted_iota(jnp.int32, (LANES, LANES), 0) == lax.broadcasted_iota(
        jnp.int32, (LANES, LANES), 1
    )


def fill_tables(place_ref, waves_ref, sites, cos_ref, sin_ref, eye):
    for axis in range(3):
        sites[axis] = column_of(place_ref[axis], eye)
    step_rows = 32

    def per_block(block, carry):
        lanes = pl.ds(pl.multiple_of(block * LANES, LANES), LANES)

        def per_rows(part, inner):
            rows = pl.ds(pl.multiple_of(part * step_rows, step_rows), step_rows)
            phase = (
                sites[0, rows, :] * waves_ref[0:1, lanes]
                + sites[1, rows, :] * waves_ref[1:2, lanes]
                + sites[2, rows, :] * waves_ref[2:3, lanes]
            )
            sine, cosine = sine_cosine(phase)
            cos_ref[block, rows, :] = cosine
            sin_ref[block, rows, :] = sine
            return inner

        return lax.fori_loop(0, LANES // step_rows, per_rows, carry)

    lax.fori_loop(0, cos_ref.shape[0], per_block, 0)


def cg_kernel(
    shape,
    negative_ref,
    species_ref,
    count_ref,
    place_ref,
    stiffness_ref,
    waves_ref,
    weight_ref,
    charges_ref,
    forces_ref,
    cos_ref,
    sin_ref,
    sites,
    vectors,
    mine,
    parts,
    total,
    whole,
    weighted,
    inbox,
    send_sem,
    recv_sem,
):
    core, pair, along, across, last = lines(shape)
    everyone = along + across + last
    barrier = pltpu.get_barrier_semaphore()
    for partner in everyone:
        pl.semaphore_signal(barrier, inc=1, device_id=partner, device_id_type=MESH)

    blocks = cos_ref.shape[0]
    scale = 1.0 / math.sqrt(lax.axis_size("dom") * lax.axis_size("slab") * LANES)
    eye = identity_mask()
    fill_tables(place_ref, waves_ref, sites, cos_ref, sin_ref, eye)

    species = species_ref[...]
    hardness = jnp.zeros(species.shape, F32)
    for element in range(stiffness_ref.shape[0]):
        hardness = jnp.where(species == element, stiffness_ref[element], hardness)
    slots = lax.broadcasted_iota(jnp.int32, (1, LANES), 1)
    live = slots < count_ref[0, 0]
    vectors[0] = column_of(jnp.where(live, negative_ref[...], 0.0), eye)
    vectors[1] = jnp.zeros((LANES, LANES), F32)
    vectors[2] = jnp.zeros((LANES, LANES), F32)
    vectors[3] = column_of(hardness, eye)
    vectors[4] = column_of(jnp.where(live, 1.0, 0.0), eye)
    mine[...] = jnp.zeros_like(mine)
    total[...] = jnp.zeros_like(total)

    pl.semaphore_wait(barrier, len(everyone))

    stages = ([pair], along, across, last)

    def copy(turn, number, source, target):
        return pltpu.make_async_remote_copy(
            src_ref=source,
            dst_ref=inbox.at[turn, number],
            send_sem=send_sem.at[number],
            recv_sem=recv_sem.at[turn, number],
            device_id=target,
            device_id_type=MESH,
        )

    def global_sum(turn):
        started = []

        def stage(targets, source):
            base = len(started)
            now = [copy(turn, base + i, source, target) for i, target in enumerate(targets)]
            for item in now:
                item.start()
            started.extend(now)
            return base, now

        base, now = stage([pair], mine.at[1 - core])
        held = mine[core]
        now[0].wait_recv()
        held = held + inbox[turn, base]
        for number, targets in enumerate((along, across)):
            parts[number] = held
            base, now = stage(targets, parts.at[number])
            for i, item in enumerate(now):
                item.wait_recv()
                held = held + inbox[turn, base + i]
        parts[2] = held
        base, now = stage(last, parts.at[2])
        other = jnp.zeros_like(held)
        for i, item in enumerate(now):
            item.wait_recv()
            if (i + 1) % 2 == 0:
                held = held + inbox[turn, base + i]
            else:
                other = other + inbox[turn, base + i]
        for item in started:
            item.wait_send()
        even = core == 0
        whole[0] = jnp.where(even, held, other)
        whole[1] = jnp.where(even, other, held)

    def iteration(turn, carry):
        previous_norm, stiff_part = carry
        residual, hard = vectors[0], vectors[3]
        hard_residual = hard * residual

        def project(block, inner):
            row = pl.ds(block, 1)
            mine[0, row, :] = jnp.sum(cos_ref[block] * residual, axis=0, keepdims=True)
            mine[1, row, :] = jnp.sum(sin_ref[block] * residual, axis=0, keepdims=True)
            return inner

        lax.fori_loop(0, blocks, project, 0)
        scalars = (residual * residual, hard_residual * residual, hard_residual * vectors[1])
        for i, product in enumerate(scalars):
            mine[0, blocks + i : blocks + i + 1, :] = jnp.sum(product, axis=0, keepdims=True)
        global_sum(turn)
        norm = whole[0, blocks : blocks + 1, :]
        beta = jnp.where(turn > 0, norm / previous_norm, 0.0)
        stiff_part = (
            whole[0, blocks + 1 : blocks + 2, :]
            + 2.0 * beta * whole[0, blocks + 2 : blocks + 3, :]
            + beta * beta * stiff_part
        )
        weight = weight_ref[...]
        recip = jnp.zeros_like(weight)
        for part in range(2):
            factors = whole[part, 0:blocks, :] + beta * total[part, 0:blocks, :]
            total[part, 0:blocks, :] = factors
            weighted[part] = weight * factors
            recip = recip + weight * factors * factors
        recip = jnp.sum(jnp.sum(recip, axis=0, keepdims=True), axis=1, keepdims=True)
        step = norm / (stiff_part + scale * recip)
        direction = residual + beta * vectors[1]
        vectors[1] = direction

        def back(block, acc):
            row = pl.ds(block, 1)
            return acc + cos_ref[block] * weighted[0, row, :] + sin_ref[block] * weighted[1, row, :]

        image = lax.fori_loop(0, blocks, back, jnp.zeros((LANES, LANES), F32))
        image = hard * direction + scale * jnp.sum(image, axis=1, keepdims=True)
        image = vectors[4] * image
        vectors[2] = vectors[2] + step * direction
        vectors[0] = residual - step * image
        for part in range(2):
            total[2 + part] = total[2 + part] + step * weighted[part]
        return norm, stiff_part

    ones = jnp.ones((1, LANES), F32)
    lax.fori_loop(0, ITERS, iteration, (ones, ones))

    charges = vectors[2]
    charges_ref[...] = row_of(charges, eye)
    half = LANES // 2
    for part in range(2):
        rows = pl.ds(part * half, half)

        def field(block, acc):
            row = pl.ds(block, 1)
            lanes = pl.ds(pl.multiple_of(block * LANES, LANES), LANES)
            term = sin_ref[block, rows, :] * total[2, row, :] - cos_ref[block, rows, :] * total[3, row, :]
            return tuple(acc[axis] + term * waves_ref[axis : axis + 1, lanes] for axis in range(3))

        zero = jnp.zeros((half, LANES), F32)
        field_parts = lax.fori_loop(0, blocks, field, (zero, zero, zero))
        for axis in range(3):
            column = scale * jnp.sum(field_parts[axis], axis=1, keepdims=True)
            sites[axis, rows, :] = jnp.broadcast_to(column, (half, LANES))
    for axis in range(3):
        forces_ref[axis] = row_of(charges * sites[axis], eye)


def equilibrate(shape, negative, species, count, place, stiffness, waves, weight):
    blocks = waves.shape[1] // LANES
    chips_x, ring, _ = shape
    copies = 1 + 2 * (ring - 1) + 2 * chips_x - 1
    vmem = pl.BlockSpec(memory_space=pltpu.VMEM)
    smem = pl.BlockSpec(memory_space=pltpu.SMEM)
    return pl.pallas_call(
        lambda *refs: cg_kernel(shape, *refs),
        name="equilibrate",
        out_shape=(
            jax.ShapeDtypeStruct((1, LANES), F32),
            jax.ShapeDtypeStruct((3, 1, LANES), F32),
        ),
        in_specs=[vmem, vmem, smem, vmem, smem, vmem, vmem],
        out_specs=(vmem, vmem),
        scratch_shapes=[
            pltpu.VMEM((blocks, LANES, LANES), F32),
            pltpu.VMEM((blocks, LANES, LANES), F32),
            pltpu.VMEM((3, LANES, LANES), F32),
            pltpu.VMEM((5, LANES, LANES), F32),
            pltpu.VMEM((2, blocks + 8, LANES), F32),
            pltpu.VMEM((3, blocks + 8, LANES), F32),
            pltpu.VMEM((4, blocks, LANES), F32),
            pltpu.VMEM((2, blocks + 8, LANES), F32),
            pltpu.VMEM((2, blocks, LANES), F32),
            pltpu.VMEM((ITERS, copies, blocks + 8, LANES), F32),
            pltpu.SemaphoreType.DMA((copies,)),
            pltpu.SemaphoreType.DMA((ITERS, copies)),
        ],
        compiler_params=pltpu.CompilerParams(
            collective_id=1, has_side_effects=True, vmem_limit_bytes=48 * 1024 * 1024
        ),
    )(negative, species, count, place, stiffness, waves, weight.reshape(blocks, LANES))


def extended(cells, sides, width):
    for axis, dim in sides:
        count = lax.axis_size(axis)
        head = lax.slice_in_dim(cells, 0, width, axis=dim)
        tail = lax.slice_in_dim(cells, cells.shape[dim] - width, cells.shape[dim], axis=dim)
        cells = jnp.concatenate(
            [
                lax.ppermute(tail, axis, [(i, (i + 1) % count) for i in range(count)]),
                cells,
                lax.ppermute(head, axis, [((i + 1) % count, i) for i in range(count)]),
            ],
            axis=dim,
        )
    return cells


def project_values(row_block, degree_channel_mixer):
    pieces = []
    for degree in range(degree_channel_mixer.shape[0]):
        first_comp = degree * degree
        last_comp = (degree + 1) * (degree + 1)
        product_part = jnp.einsum(
            "ncd,de->nce",
            row_block[:, first_comp:last_comp, :],
            degree_channel_mixer[degree],
            preferred_element_type=jnp.float32,
        )
        pieces.append(product_part.astype(jnp.bfloat16))
    joined = jnp.concatenate(pieces, axis=1)
    return joined.reshape(row_block.shape[0], -1)


def readout_sum(message, affinity_output_head):
    result_sum = jnp.sum(message[:, 0, :] * affinity_output_head[0], axis=1)
    for degree in range(1, affinity_output_head.shape[0]):
        first_comp = degree * degree
        last_comp = (degree + 1) * (degree + 1)
        part_sq = message[:, first_comp:last_comp, :] * message[:, first_comp:last_comp, :]
        channel_norm = jnp.sqrt(jnp.sum(part_sq, axis=1) + 1e-06)
        result_sum = result_sum + jnp.sum(channel_norm * affinity_output_head[degree], axis=1)
    return result_sum


def shards(
    equivariant_embedding,
    cartesian_coordinates,
    element_identity,
    occupied_site_totals,
    halo_export_indices,
    adjacency_rows,
    attention_source_weights,
    attention_target_weights,
    degree_channel_mixer,
    affinity_output_head,
    baseline_affinity_per_element,
    chemical_stiffness,
    reciprocal_lattice_points,
    ewald_weighting,
):
    atom_slots = equivariant_embedding.shape[2]
    channels = equivariant_embedding.shape[4]
    own_feats = equivariant_embedding[0, 0]
    scalar_ch = own_feats[:, 0, :]
    queries = jnp.dot(
        scalar_ch, attention_source_weights, preferred_element_type=jnp.float32
    ).astype(jnp.bfloat16)
    own_keys = jnp.dot(
        scalar_ch, attention_target_weights, preferred_element_type=jnp.float32
    ).astype(jnp.bfloat16)
    own_values = project_values(own_feats, degree_channel_mixer)
    packed = jnp.concatenate([own_keys, own_values], axis=1)
    outgoing = packed[halo_export_indices[0, 0]]
    arrived = extended(outgoing[None, None], (("dom", 0), ("slab", 1)), 1)
    arrived = arrived.reshape(-1, packed.shape[1])
    table_keys = jnp.concatenate([own_keys, arrived[:, :channels]], axis=0)
    table_values = jnp.concatenate([own_values, arrived[:, channels:]], axis=0)
    table_size = table_keys.shape[0]
    neigh_dev = adjacency_rows[0, 0]
    columns = jnp.arange(table_size, dtype=jnp.int32)
    neighbour_mask = jnp.any(neigh_dev[:, :, None] == columns[None, None, :], axis=1)
    scores = jnp.einsum("ac,tc->at", queries, table_keys, preferred_element_type=jnp.float32)
    weights = jnp.where(
        neighbour_mask, jax.nn.sigmoid(scores / math.sqrt(channels)) * 0.125, 0.0
    ).astype(jnp.bfloat16)
    message = jnp.dot(weights, table_values, preferred_element_type=jnp.float32).reshape(
        atom_slots, -1, channels
    )
    element_hit = (
        element_identity[0, 0][:, None]
        == jnp.arange(baseline_affinity_per_element.shape[0], dtype=jnp.int32)[None, :]
    ).astype(jnp.float32)
    electroneg = readout_sum(message, affinity_output_head) + jnp.sum(
        element_hit * baseline_affinity_per_element[None, :], axis=1
    )
    chips_x = CHIPS_X
    chips_z = lax.axis_size("dom") // chips_x
    chips_y = lax.axis_size("slab") // 2
    charges, forces = equilibrate(
        (chips_x, chips_y, chips_z),
        (-electroneg).reshape(1, atom_slots),
        element_identity[0],
        occupied_site_totals,
        cartesian_coordinates[0, 0].reshape(3, 1, atom_slots),
        chemical_stiffness,
        reciprocal_lattice_points,
        ewald_weighting,
    )
    return (charges.reshape(1, 1, atom_slots), forces.reshape(1, 1, 3, atom_slots))


def solution(mesh):
    placed = (
        P("dom", "slab", None, None, None),
        P("dom", "slab", None, None),
        P("dom", "slab", None),
        P("dom", "slab"),
        P("dom", "slab", None),
        P("dom", "slab", None, None),
        P(),
        P(),
        P(),
        P(),
        P(),
        P(),
        P(),
        P(),
    )
    return jax.shard_map(
        shards,
        mesh=mesh,
        in_specs=placed,
        out_specs=(P("dom", "slab", None), P("dom", "slab", None, None)),
        check_vma=False,
    )
```

time: 1410 us -> 135 us (0.10)
  blocking collectives: 1150 us -> 0 us
  matrix products: 183 us -> 10.2 us
  Pallas kernels: 0 us -> 83.9 us
  local copies, waits for them, and re-layouts: 33.2 us -> 2.8 us
    psum x12 -> x0, blocking collectives: 1150 us -> none  [the longest x4 383 us: shards(): cos_sum, sin_sum = lax.psum((dir_cos, dir_sin), ('dom', 'slab'))]
    dot_general x20 -> x0, matrix products: 173 us -> none  [the longest x5 42 us: local_factors(): jnp.dot(vector_in, odd_harmonic_entries, precision=highest_accuracy_mode)]
    pallas_call x0 -> x1, Pallas kernels: none -> 83.9 us  [equilibrate(): pl.pallas_call(lambda *refs: cg_kernel(shape, *refs), name='equilibrate',...]
    unnamed x33 -> x24, local copies, waits for them, and re-layouts: 31.5 us -> 1.15 us
  transfers between devices with their start and end apart: 4 -> 4, of which waited for: 2 -> 4; matrix products, arithmetic and copies ran while one was open for 2% -> 2% of each run, Pallas kernels for 0% -> 0%
where the time goes in v1:
time: 135 us
  Pallas kernels  83.9 us (62%)
  starting transfers between devices  18.3 us (14%)
  matrix products  10.2 us (8%)
  waiting for transfers between devices  9.76 us (7%)
  other arithmetic  8.13 us (6%)
  local copies, waits for them, and re-layouts  2.8 us (2%)
  between operations  1.55 us (1%)
    pallas_call x1, Pallas kernels, equilibrate(): pl.pallas_call(lambda *refs: cg_kernel(shape, *refs), name='equilibrate',...  83.9 us
    ppermute x2, starting transfers between devices, extended(): lax.ppermute(head, axis, [((i + 1) % count, i) for i in range(count)])  10.8 us
    ppermute x2, starting transfers between devices, extended(): lax.ppermute(tail, axis, [(i, (i + 1) % count) for i in range(count)])  7.55 us
    ppermute x2, waiting for transfers between devices, extended(): lax.ppermute(tail, axis, [(i, (i + 1) % count) for i in range(count)])  6.38 us
    dot_general x5, matrix products, project_values(): jnp.einsum('ncd,de->nce', row_block[:, first_comp:last_comp, :], degree_c...  5.78 us
    reduce_sum x4, other arithmetic, readout_sum(): channel_norm = jnp.sqrt(jnp.sum(part_sq, axis=1) + 1e-06)  4.19 us
    ppermute x2, waiting for transfers between devices, extended(): lax.ppermute(head, axis, [((i + 1) % count, i) for i in range(count)])  3.38 us
  transfers between devices with their start and end apart: 4, of which 4 were waited for; matrix products, arithmetic and copies ran while one was open for 2% of the time, Pallas kernels for 0%

profile of v1, /device:TPU:1, one launch (start us, length us, event | category | flops | bytes accessed | tf_op | source)
XLA Modules:
  0.0 134.7 jit_solution(12168234490561641440)
XLA Ops:
  0.6 0.0 copy-start
  0.6 0.0 copy-start.9
  0.7 1.0 fusion.17
  1.7 1.1 fusion.15
  2.8 1.2 fusion.7
  4.0 1.2 fusion.6
  5.2 1.3 fusion.5
  6.5 0.8 copy.46
  7.3 0.0 copy-done
  7.3 0.9 convolution_convert_fusion.5
  8.2 0.0 copy-done.9
  8.3 0.1 pad_maximum_fusion.1
  8.3 0.0 copy-start.8
  8.3 0.0 copy-start.4
  8.3 0.0 copy-start.10
  8.4 0.0 copy-start.6
  8.4 0.0 copy-start.7
  8.4 0.7 gather_fusion
  9.1 4.8 %collective-permute-start = (bf16[1,1,32,3328]{3,2,1,0:T(8,128)(2,1)S(1)}, bf16[1,1,32,3328]{3,2,1,0:T(8,128)(2,1)S(1)}, u32[]{:S(2)}, u32[]{:S(2)}) collective-permute-start(bf16[1,1,32,3328]{3,2,1,0:T(8,128)(2,1)S(1)} %bitcast.87), channel_id=1, source_target_pairs={{0,16},{16,32},{32,48},{48,64},{64,80},{80,96},{96,112},{112,128},... | collective-permute-start | bytes 638984 | tf_op jit(solution)/shard_map/ppermute | solution.py:318
  13.9 10.8 %collective-permute-start.1 = (bf16[1,1,32,3328]{3,2,1,0:T(8,128)(2,1)S(1)}, bf16[1,1,32,3328]{3,2,1,0:T(8,128)(2,1)S(1)}, u32[]{:S(2)}, u32[]{:S(2)}) collective-permute-start(bf16[1,1,32,3328]{3,2,1,0:T(8,128)(2,1)S(1)} %bitcast.88), channel_id=1, source_target_pairs={{16,0},{32,16},{48,32},{64,48},{80,64},{96,80},{112,96},{128,112},... | collective-permute-start | bytes 638984 | tf_op jit(solution)/shard_map/ppermute | solution.py:320
  24.7 3.0 %collective-permute-done = bf16[1,1,32,3328]{3,2,1,0:T(8,128)(2,1)S(1)} collective-permute-done((bf16[1,1,32,3328]{3,2,1,0:T(8,128)(2,1)S(1)}, bf16[1,1,32,3328]{3,2,1,0:T(8,128)(2,1)S(1)}, u32[]{:S(2)}, u32[]{:S(2)}) %collective-permute-start) | collective-permute-done | bytes 213024 | tf_op jit(solution)/shard_map/ppermute | solution.py:318
  27.7 0.9 collective-permute-done.1
  28.6 0.1 pad_maximum_fusion.2
  28.7 2.7 %collective-permute-start.2 = (bf16[3,1,32,3328]{3,2,1,0:T(8,128)(2,1)S(1)}, bf16[3,1,32,3328]{3,2,1,0:T(8,128)(2,1)S(1)}, u32[]{:S(2)}, u32[]{:S(2)}) collective-permute-start(bf16[3,1,32,3328]{3,2,1,0:T(8,128)(2,1)S(1)} %pad_maximum_fusion.2), channel_id=1, source_target_pairs={{0,1},{1,2},{2,3},{3,4},{4,5},{5,6},{6,7},{7,8},{8,9},{9,10},{10,1... | collective-permute-start | bytes 1916936 | tf_op jit(solution)/shard_map/ppermute | solution.py:318
  31.4 0.0 collective-permute-start.3
  31.4 0.0 copy-done.8
  32.1 0.0 copy-done.4
  32.1 0.0 copy-done.10
  32.1 0.1 select_reduce_fusion
  32.2 0.0 copy-done.6
  32.2 0.9 convolution_convert_fusion.6
  33.1 0.0 copy-done.7
  33.1 2.3 %fusion = pred[128,416]{0,1:T(8,128)(4,1)S(1)} fusion(s32[128,64]{0,1:T(8,128)S(1)} %bitcast.100), kind=kLoop, calls=%fused_computation.2 | loop fusion | flops 6762496 | bytes 86016 | tf_op jit(solution)/shard_map/reduce_or | solution.py:390
  35.4 3.4 %collective-permute-done.2 = bf16[3,1,32,3328]{3,2,1,0:T(8,128)(2,1)S(1)} collective-permute-done((bf16[3,1,32,3328]{3,2,1,0:T(8,128)(2,1)S(1)}, bf16[3,1,32,3328]{3,2,1,0:T(8,128)(2,1)S(1)}, u32[]{:S(2)}, u32[]{:S(2)}) %collective-permute-start.2) | collective-permute-done | bytes 639008 | tf_op jit(solution)/shard_map/ppermute | solution.py:318
  38.8 2.5 %collective-permute-done.3 = bf16[3,1,32,3328]{3,2,1,0:T(8,128)(2,1)S(1)} collective-permute-done((bf16[3,1,32,3328]{3,2,1,0:T(8,128)(2,1)S(1)}, bf16[3,1,32,3328]{3,2,1,0:T(8,128)(2,1)S(1)}, u32[]{:S(2)}, u32[]{:S(2)}) %collective-permute-start.3) | collective-permute-done | bytes 639008 | tf_op jit(solution)/shard_map/ppermute | solution.py:320
  41.2 0.2 pad_maximum_fusion
  41.5 0.1 slice.97
  41.6 2.6 %fusion.1 = f32[128,3200]{0,1:T(8,128)} fusion(bf16[288,3200]{1,0:T(8,128)(2,1)S(1)} %slice.97, bf16[128,3200]{1,0:T(8,128)(2,1)S(1)} %copy.46, pred[128,416]{0,1:T(8,128)(4,1)S(1)} %fusion, bf16[128,128]{1,0:T(8,128)(2,1)S(1)} %convolution_convert_fusion.6, bf16[288,128]{1,0:T(8,128)(2,1)S(1)} %slice.96, bf16[128,128]{1,0:T(8,128)(2,1)S(1)} %convolution_convert_fusion.5), kind=kOutput, calls=%fused_computation.3 | convolution fusion | flops 360329216 | bytes 4493312 | tf_op jit(solution)/shard_map/dot_general | solution.py:395
  44.3 0.0 copy-start.1
  44.3 0.0 copy-start.2
  44.3 0.0 copy-start.3
  44.3 0.0 copy-start.5
  44.3 1.1 fusion.19
  45.4 1.0 fusion.20
  46.4 1.1 fusion.18
  47.5 1.0 fusion.21
  48.5 0.1 multiply_reduce_fusion.3
  48.6 1.0 fusion.33
  49.5 0.1 multiply_reduce_fusion.1
  49.6 0.0 copy-done.1
  49.7 0.0 copy-done.2
  49.7 0.0 copy-done.3
  49.7 0.0 copy-done.5
  49.7 83.9 %equilibrate.1 = (f32[1,128]{1,0:T(1,128)S(1)}, f32[3,1,128]{2,1,0:T(1,128)S(1)}) custom-call(f32[1,128]{1,0:T(1,128)S(1)} %negate_bitcast_fusion.refs_0_, s32[1,128]{1,0:T(1,128)S(1)} %bitcast.83, s32[1,1]{1,0:T(1,128)S(6)} %copy.61.refs_2_, f32[3,1,128]{2,1,0:T(1,128)S(1)} %bitcast.81, f32[4]{0:T(128)S(1)} %copy-done.5, f32[3,4096]{1,0:T(4,128)S(1)} %copy-done.1, ...), custom_call_target="tpu_custom_call" | custom-call | tf_op jit(solution)/shard_map/equilibrate/pallas_call | solution.py:282
  133.6 0.5 copy.62
  134.1 0.6 copy.63
  (5 shorter events, 0.0 us)
Async XLA Ops:
  0.6 6.7 %copy-start = (bf16[128,128]{1,0:T(8,128)(2,1)S(1)}, bf16[128,128]{1,0:T(8,128)(2,1)}, u32[]{:S(2)}) copy-start(bf16[128,128]{1,0:T(8,128)(2,1)} %param.21) | copy-start | bytes 98308
  0.6 7.6 %copy-start.9 = (s32[1,1,32]{2,1,0:T(1,128)S(1)}, s32[1,1,32]{2,1,0:T(1,128)}, u32[]{:S(2)}) copy-start(s32[1,1,32]{2,1,0:T(1,128)} %param.18) | copy-start | bytes 388
  8.3 23.1 %copy-start.8 = (f32[5,128]{1,0:T(8,128)S(1)}, f32[5,128]{1,0:T(8,128)}, u32[]{:S(2)}) copy-start(f32[5,128]{1,0:T(8,128)} %param.23) | copy-start | bytes 7684
  8.3 23.7 %copy-start.4 = (s32[1,1,128]{2,1,0:T(1,128)S(1)}, s32[1,1,128]{2,1,0:T(1,128)}, u32[]{:S(2)}) copy-start(s32[1,1,128]{2,1,0:T(1,128)} %param.16) | copy-start | bytes 1540
  8.3 23.7 %copy-start.10 = (f32[4]{0:T(128)S(1)}, f32[4]{0:T(128)}, u32[]{:S(2)}) copy-start(f32[4]{0:T(128)} %param.24) | copy-start | bytes 52
  8.4 23.8 %copy-start.6 = (bf16[128,128]{1,0:T(8,128)(2,1)S(1)}, bf16[128,128]{1,0:T(8,128)(2,1)}, u32[]{:S(2)}) copy-start(bf16[128,128]{1,0:T(8,128)(2,1)} %param.20) | copy-start | bytes 98308
  8.4 24.7 %copy-start.7 = (s32[1,1,128,64]{2,3,1,0:T(8,128)S(1)}, s32[1,1,128,64]{2,3,1,0:T(8,128)}, u32[]{:S(2)}) copy-start(s32[1,1,128,64]{2,3,1,0:T(8,128)} %param.19) | copy-start | bytes 98308
  9.1 18.6 %collective-permute-start = (bf16[1,1,32,3328]{3,2,1,0:T(8,128)(2,1)S(1)}, bf16[1,1,32,3328]{3,2,1,0:T(8,128)(2,1)S(1)}, u32[]{:S(2)}, u32[]{:S(2)}) collective-permute-start(bf16[1,1,32,3328]{3,2,1,0:T(8,128)(2,1)S(1)} %bitcast.87), channel_id=1, source_target_pairs={{0,16},{16,32},{32,48},{48,64},{64,80},{80,96},{96,112},{112,128},... | collective-permute-start | bytes 638984 | tf_op jit(solution)/shard_map/ppermute | solution.py:318
  13.9 14.7 %collective-permute-start.1 = (bf16[1,1,32,3328]{3,2,1,0:T(8,128)(2,1)S(1)}, bf16[1,1,32,3328]{3,2,1,0:T(8,128)(2,1)S(1)}, u32[]{:S(2)}, u32[]{:S(2)}) collective-permute-start(bf16[1,1,32,3328]{3,2,1,0:T(8,128)(2,1)S(1)} %bitcast.88), channel_id=1, source_target_pairs={{16,0},{32,16},{48,32},{64,48},{80,64},{96,80},{112,96},{128,112},... | collective-permute-start | bytes 638984 | tf_op jit(solution)/shard_map/ppermute | solution.py:320
  28.7 10.1 %collective-permute-start.2 = (bf16[3,1,32,3328]{3,2,1,0:T(8,128)(2,1)S(1)}, bf16[3,1,32,3328]{3,2,1,0:T(8,128)(2,1)S(1)}, u32[]{:S(2)}, u32[]{:S(2)}) collective-permute-start(bf16[3,1,32,3328]{3,2,1,0:T(8,128)(2,1)S(1)} %pad_maximum_fusion.2), channel_id=1, source_target_pairs={{0,1},{1,2},{2,3},{3,4},{4,5},{5,6},{6,7},{7,8},{8,9},{9,10},{10,1... | collective-permute-start | bytes 1916936 | tf_op jit(solution)/shard_map/ppermute | solution.py:318
  31.4 9.8 %collective-permute-start.3 = (bf16[3,1,32,3328]{3,2,1,0:T(8,128)(2,1)S(1)}, bf16[3,1,32,3328]{3,2,1,0:T(8,128)(2,1)S(1)}, u32[]{:S(2)}, u32[]{:S(2)}) collective-permute-start(bf16[3,1,32,3328]{3,2,1,0:T(8,128)(2,1)S(1)} %pad_maximum_fusion.2), channel_id=1, source_target_pairs={{1,0},{2,1},{3,2},{4,3},{5,4},{6,5},{7,6},{8,7},{9,8},{10,9},{11,1... | collective-permute-start | bytes 1916936 | tf_op jit(solution)/shard_map/ppermute | solution.py:320
  44.3 5.4 %copy-start.1 = (f32[3,4096]{1,0:T(4,128)S(1)}, f32[3,4096]{1,0:T(4,128)}, u32[]{:S(2)}) copy-start(f32[3,4096]{1,0:T(4,128)} %refs_5_.1) | copy-start | bytes 147460
  44.3 5.4 %copy-start.2 = (f32[4096]{0:T(1024)S(1)}, f32[4096]{0:T(1024)}, u32[]{:S(2)}) copy-start(f32[4096]{0:T(1024)} %param.27) | copy-start | bytes 49156
  44.3 5.4 %copy-start.3 = (f32[1,1,3,128]{3,1,2,0:T(1,128)S(1)}, f32[1,1,3,128]{3,1,2,0:T(1,128)}, u32[]{:S(2)}) copy-start(f32[1,1,3,128]{3,1,2,0:T(1,128)} %param.15) | copy-start | bytes 4612
  44.3 5.4 %copy-start.5 = (f32[4]{0:T(128)S(1)}, f32[4]{0:T(128)}, u32[]{:S(2)}) copy-start(f32[4]{0:T(128)} %refs_4_.1) | copy-start | bytes 52

commit v2 on v1

v2 whole, which is shorter than its diff:
```python
import math

import jax
import jax.numpy as jnp
from jax import lax
from jax.experimental import pallas as pl
from jax.experimental.pallas import tpu as pltpu
from jax.sharding import PartitionSpec as P

ITERS = 4
CHIPS_X = 4
LANES = 128
MESH = pl.DeviceIdType.MESH
F32 = jnp.float32

HALF_PI_PARTS = (1.5703125, 4.837512969970703125e-4, 7.54978995489188216e-8)


def sine_cosine(phase):
    quadrant = jnp.round(phase * (2.0 / math.pi))
    reduced = phase - quadrant * HALF_PI_PARTS[0]
    reduced = reduced - quadrant * HALF_PI_PARTS[1]
    reduced = reduced - quadrant * HALF_PI_PARTS[2]
    square = reduced * reduced
    odd = (-1.9515295891e-4 * square + 8.3321608736e-3) * square - 1.6666654611e-1
    odd = odd * square * reduced + reduced
    even = (2.443315711809948e-5 * square - 1.388731625493765e-3) * square
    even = (even + 4.166664568298827e-2) * square * square - 0.5 * square + 1.0
    turn = quadrant.astype(jnp.int32)
    swap = (turn & 1) == 1
    sine = jnp.where(swap, even, odd)
    cosine = jnp.where(swap, odd, even)
    sine = jnp.where((turn & 2) == 2, -sine, sine)
    cosine = jnp.where(((turn + 1) & 2) == 2, -cosine, cosine)
    return sine, cosine


CHUNKS = 2
SCALARS = 3


def place_of(shape):
    chips_x, chips_y, chips_z = shape
    dom, slab = lax.axis_index("dom"), lax.axis_index("slab")
    return dom // chips_z, slab // 2, dom % chips_z, slab % 2


def device(shape, x, y, z, core):
    return (x * shape[2] + z, y * 2 + core)


def far_first(count):
    return sorted(range(1, count), key=lambda j: -min(j, count - j))


def sum_partners(shape):
    x, y, z, core = place_of(shape)
    chips_x, ring, _ = shape
    group = 2 * chips_x
    mine = x * 2 + core
    peers = []
    for i in far_first(group):
        other = (mine + i) % group
        peers.append((other, device(shape, other // 2, y, z, other % 2)))
    along = [
        device(shape, x, (y + j * (1 - core)) % ring, (z + j * core) % ring, core)
        for j in far_first(ring)
    ]
    across = [
        device(shape, x, (y + j * core) % ring, (z + j * (1 - core)) % ring, core)
        for j in far_first(ring)
    ]
    return mine, peers, along, across


def halo_partners(shape):
    x, y, z, core = place_of(shape)
    domains = shape[0] * shape[2]
    dom, slab = lax.axis_index("dom"), lax.axis_index("slab")
    way = 1 - 2 * core
    return {
        "before": ((dom + domains - 1) % domains, slab),
        "after": ((dom + 1) % domains, slab),
        "pair": (dom, y * 2 + 1 - core),
        "outer": (dom, (slab + 2 * shape[1] - way) % (2 * shape[1])),
        "ahead": ((dom + domains + way) % domains, slab),
    }


def row_of(column, eye):
    return jnp.sum(jnp.where(eye, column, 0.0), axis=0, keepdims=True)


def column_of(row, eye):
    wide = jnp.broadcast_to(row, (LANES, LANES))
    return jnp.broadcast_to(
        jnp.sum(jnp.where(eye, wide, 0.0), axis=1, keepdims=True), (LANES, LANES)
    )


def identity_mask(count):
    shape = (count, count)
    return lax.broadcasted_iota(jnp.int32, shape, 0) == lax.broadcasted_iota(jnp.int32, shape, 1)


def degrees_of(comps):
    return [range(l * l, (l + 1) * (l + 1)) for l in range(math.isqrt(comps))]


def fill_tables(first, stop, waves_ref, sites, cos_ref, sin_ref):
    step_rows = 32

    def per_block(block, carry):
        lanes = pl.ds(pl.multiple_of(block * LANES, LANES), LANES)

        def per_rows(part, inner):
            rows = pl.ds(pl.multiple_of(part * step_rows, step_rows), step_rows)
            phase = (
                sites[0, rows, :] * waves_ref[0:1, lanes]
                + sites[1, rows, :] * waves_ref[1:2, lanes]
                + sites[2, rows, :] * waves_ref[2:3, lanes]
            )
            sine, cosine = sine_cosine(phase)
            cos_ref[block, rows, :] = cosine
            sin_ref[block, rows, :] = sine
            return inner

        return lax.fori_loop(0, LANES // step_rows, per_rows, carry)

    lax.fori_loop(first, stop, per_block, 0)


def fill_mask(adjacency_ref, upright, mask_ref):
    size = upright.shape[0]
    ghosts = (size - LANES) // 8
    group = 64

    def per_group(part, carry):
        start = part * group
        row = lax.broadcasted_iota(jnp.int32, (group, LANES), 0) + start
        row = row + jnp.where(row >= LANES + 4 * ghosts, ghosts, 0)
        hit = row == adjacency_ref[0:1, :]
        for j in range(1, adjacency_ref.shape[0]):
            hit = hit | (row == adjacency_ref[j : j + 1, :])
        upright[pl.ds(pl.multiple_of(start, group), group), :] = jnp.where(hit, 1.0, 0.0)
        return carry

    lax.fori_loop(0, size // group, per_group, 0)
    for part in range(size // LANES):
        span = slice(part * LANES, (part + 1) * LANES)
        mask_ref[:, span] = upright[span, :].T


def attention(queries, keys, mask):
    scores = lax.dot_general(
        queries, keys, (((1,), (1,)), ((), ())), preferred_element_type=F32
    )
    gate = jax.nn.sigmoid(scores / math.sqrt(LANES)) * 0.125
    return jnp.where(mask > 0.0, gate, 0.0).astype(jnp.bfloat16)


def whole_kernel(
    shape,
    features_ref,
    place_ref,
    species_ref,
    count_ref,
    export_ref,
    adjacency_ref,
    source_ref,
    target_ref,
    mixer_ref,
    head_ref,
    baseline_ref,
    stiffness_ref,
    waves_ref,
    weight_ref,
    charges_ref,
    forces_ref,
    queries,
    table,
    outgoing,
    arrived,
    upright,
    mask_ref,
    own_message,
    cos_ref,
    sin_ref,
    sites,
    vectors,
    mine,
    parts,
    inbox,
    whole,
    total,
    weighted,
    halo_send,
    halo_recv,
    send_sem,
    recv_sem,
):
    group_index, peers, along, across = sum_partners(shape)
    near = halo_partners(shape)
    core = place_of(shape)[3]
    group = len(peers) + 1
    everyone = [peer for _, peer in peers] + along + across
    everyone += [near[name] for name in ("before", "after", "pair", "outer")]
    barrier = pltpu.get_barrier_semaphore()
    for partner in everyone:
        pl.semaphore_signal(barrier, inc=1, device_id=partner, device_id_type=MESH)

    comps = features_ref.shape[0]
    ghosts = outgoing.shape[1]
    blocks = cos_ref.shape[0]
    scale = 1.0 / math.sqrt(lax.axis_size("dom") * lax.axis_size("slab") * LANES)
    bf16 = jnp.bfloat16

    for degree, span in enumerate(degrees_of(comps)):
        for comp in span:
            product = jnp.dot(
                features_ref[comp], mixer_ref[degree], preferred_element_type=F32
            )
            table[comp] = product.astype(bf16)
    scalar = features_ref[0]
    table[comps] = jnp.dot(scalar, target_ref[...], preferred_element_type=F32).astype(bf16)
    queries[...] = jnp.dot(scalar, source_ref[...], preferred_element_type=F32).astype(bf16)
    offered = jnp.broadcast_to(export_ref[...], (ghosts, ghosts)).astype(F32)
    offered = jnp.sum(jnp.where(identity_mask(ghosts), offered, 0.0), axis=1, keepdims=True)
    slots = lax.broadcasted_iota(jnp.int32, (ghosts, LANES), 1).astype(F32)
    pick = jnp.where(slots == offered, 1.0, 0.0).astype(bf16)
    for comp in range(comps + 1):
        row = jnp.dot(pick, table[comp], preferred_element_type=F32)
        outgoing[comp] = row.astype(bf16)

    eye = identity_mask(LANES)
    for axis in range(3):
        sites[axis] = column_of(place_ref[axis], eye)
    species = species_ref[...]
    hardness = jnp.zeros(species.shape, F32)
    baseline = jnp.zeros(species.shape, F32)
    for element in range(stiffness_ref.shape[0]):
        hardness = jnp.where(species == element, stiffness_ref[element], hardness)
        baseline = jnp.where(species == element, baseline_ref[element], baseline)
    live = lax.broadcasted_iota(jnp.int32, (1, LANES), 1) < count_ref[0, 0]
    vectors[0] = column_of(baseline, eye)
    vectors[1] = jnp.zeros((LANES, LANES), F32)
    vectors[2] = jnp.zeros((LANES, LANES), F32)
    vectors[3] = column_of(hardness, eye)
    vectors[4] = column_of(jnp.where(live, 1.0, 0.0), eye)
    total[...] = jnp.zeros_like(total)

    pl.semaphore_wait(barrier, len(everyone))

    size = (comps + 1) // CHUNKS

    def ship(number, chunk, source, slot, target):
        span = pl.ds(chunk * size, size)
        return pltpu.make_async_remote_copy(
            src_ref=source,
            dst_ref=arrived.at[span, slot],
            send_sem=halo_send.at[number * CHUNKS + chunk],
            recv_sem=halo_recv.at[number * CHUNKS + chunk],
            device_id=target,
            device_id_type=MESH,
        )

    def own(chunk):
        return outgoing.at[pl.ds(chunk * size, size)]

    def got(chunk, slot):
        return arrived.at[pl.ds(chunk * size, size), slot]

    sent = {}
    for chunk in range(CHUNKS):
        sent["after", chunk] = ship(0, chunk, own(chunk), 1, near["after"])
        sent["before", chunk] = ship(1, chunk, own(chunk), 6, near["before"])
        sent["outer", chunk] = ship(2, chunk, own(chunk), 4 - core, near["outer"])
        sent["pair", chunk] = ship(3, chunk, own(chunk), 3 + core, near["pair"])
        for name in ("after", "before", "outer", "pair"):
            sent[name, chunk].start()

    fill_mask(adjacency_ref, upright, mask_ref)
    own_weights = attention(queries[...], table[comps], mask_ref[:, 0:LANES])
    for comp in range(comps):
        own_message[comp] = jnp.dot(own_weights, table[comp], preferred_element_type=F32)

    for chunk in range(CHUNKS):
        fill_tables(
            chunk * blocks // CHUNKS, (chunk + 1) * blocks // CHUNKS, waves_ref, sites, cos_ref, sin_ref
        )
        sent["outer", chunk].wait_recv()
        sent["ring", chunk] = ship(4, chunk, got(chunk, 3 + core), 7 * core, near["ahead"])
        sent["ring", chunk].start()
        sent["after", chunk].wait_recv()
        sent["before", chunk].wait_recv()
        sent["cross", chunk] = ship(5, chunk, got(chunk, 1 + 5 * core), 2 + 3 * core, near["outer"])
        sent["low", chunk] = ship(6, chunk, got(chunk, 1), 2 * core, near["pair"])
        sent["high", chunk] = ship(7, chunk, got(chunk, 6), 5 + 2 * core, near["pair"])
        for name in ("cross", "low", "high"):
            sent[name, chunk].start()
    for chunk in range(CHUNKS):
        for name in ("pair", "ring", "cross", "low", "high"):
            sent[name, chunk].wait_recv()

    ghost_keys = arrived[comps].reshape(8 * ghosts, LANES)
    weights = attention(queries[...], ghost_keys, mask_ref[:, LANES:])
    readout = jnp.zeros((LANES, LANES), F32)
    for degree, span in enumerate(degrees_of(comps)):
        square = jnp.zeros((LANES, LANES), F32)
        for comp in span:
            message = own_message[comp] + jnp.dot(
                weights, arrived[comp].reshape(8 * ghosts, LANES), preferred_element_type=F32
            )
            square = message if degree == 0 else square + message * message
        norm = square if degree == 0 else jnp.sqrt(square + 1e-06)
        readout = readout + norm * head_ref[degree : degree + 1, :]
    electroneg = jnp.sum(readout, axis=1, keepdims=True) + vectors[0]
    vectors[0] = vectors[4] * -electroneg
    for item in sent.values():
        item.wait_send()

    piece = mine.shape[1] - SCALARS
    halves = group // 2

    def copy(turn, number, source, drop, target):
        return pltpu.make_async_remote_copy(
            src_ref=source,
            dst_ref=drop,
            send_sem=send_sem.at[number],
            recv_sem=recv_sem.at[turn, number],
            device_id=target,
            device_id_type=MESH,
        )

    def global_sum(turn):
        started = []
        for other, target in peers:
            number = len(started)
            started.append(copy(turn, number, mine.at[other], inbox.at[turn, number], target))
            started[-1].start()
        held = mine[group_index]
        for number in range(len(peers)):
            started[number].wait_recv()
            held = held + inbox[turn, number]
        for stage, targets in enumerate((along, across)):
            parts[stage] = held
            first = len(started)
            for target in targets:
                number = len(started)
                started.append(copy(turn, number, parts.at[stage], inbox.at[turn, number], target))
                started[-1].start()
            for number in range(first, len(started)):
                started[number].wait_recv()
                held = held + inbox[turn, number]
        parts[2] = held
        first = len(started)
        for _, target in peers:
            number = len(started)
            drop = whole.at[turn, group_index]
            started.append(copy(turn, number, parts.at[2], drop, target))
            started[-1].start()
        whole[turn, group_index] = held
        for item in started[first:]:
            item.wait_recv()
        for item in started:
            item.wait_send()

    def iteration(turn, carry):
        previous_norm, stiff_part = carry
        residual, hard = vectors[0], vectors[3]
        hard_residual = hard * residual

        def project(part, inner):
            for j in range(piece):
                block = part * piece + j
                mine[part, j : j + 1, :] = jnp.sum(
                    cos_ref[block] * residual, axis=0, keepdims=True
                )
                mine[part + halves, j : j + 1, :] = jnp.sum(
                    sin_ref[block] * residual, axis=0, keepdims=True
                )
            return inner

        lax.fori_loop(0, halves, project, 0)
        scalars = (residual * residual, hard_residual * residual, hard_residual * vectors[1])
        for i, product in enumerate(scalars):
            row = jnp.sum(product, axis=0, keepdims=True)
            for part in range(group):
                mine[part, piece + i : piece + i + 1, :] = row
        global_sum(turn)
        norm, pure, mixed = (
            whole[turn, 0, piece + i : piece + i + 1, :] for i in range(SCALARS)
        )
        beta = jnp.where(turn > 0, norm / previous_norm, 0.0)
        stiff_part = pure + 2.0 * beta * mixed + beta * beta * stiff_part
        weight = weight_ref[...]
        recip = jnp.zeros_like(weight)
        for part in range(2):
            factors = whole[turn, pl.ds(part * halves, halves), 0:piece, :]
            factors = factors.reshape(blocks, LANES) + beta * total[part]
            total[part] = factors
            weighted[part] = weight * factors
            recip = recip + weight * factors * factors
        recip = jnp.sum(jnp.sum(recip, axis=0, keepdims=True), axis=1, keepdims=True)
        step = norm / (stiff_part + scale * recip)
        direction = residual + beta * vectors[1]
        vectors[1] = direction

        def back(part, acc):
            for j in range(2):
                block = part * 2 + j
                row = pl.ds(block, 1)
                acc = acc + cos_ref[block] * weighted[0, row, :]
                acc = acc + sin_ref[block] * weighted[1, row, :]
            return acc

        image = lax.fori_loop(0, blocks // 2, back, jnp.zeros((LANES, LANES), F32))
        image = hard * direction + scale * jnp.sum(image, axis=1, keepdims=True)
        image = vectors[4] * image
        vectors[2] = vectors[2] + step * direction
        vectors[0] = residual - step * image
        for part in range(2):
            total[2 + part] = total[2 + part] + step * weighted[part]
        return norm, stiff_part

    ones = jnp.ones((1, LANES), F32)
    lax.fori_loop(0, ITERS, iteration, (ones, ones))

    charges = vectors[2]
    charges_ref[...] = row_of(charges, eye)
    half = LANES // 2
    for part in range(2):
        rows = pl.ds(part * half, half)

        def field(block, acc):
            row = pl.ds(block, 1)
            lanes = pl.ds(pl.multiple_of(block * LANES, LANES), LANES)
            term = (
                sin_ref[block, rows, :] * total[2, row, :]
                - cos_ref[block, rows, :] * total[3, row, :]
            )
            return tuple(acc[axis] + term * waves_ref[axis : axis + 1, lanes] for axis in range(3))

        zero = jnp.zeros((half, LANES), F32)
        field_parts = lax.fori_loop(0, blocks, field, (zero, zero, zero))
        for axis in range(3):
            column = scale * jnp.sum(field_parts[axis], axis=1, keepdims=True)
            sites[axis, rows, :] = jnp.broadcast_to(column, (half, LANES))
    for axis in range(3):
        forces_ref[axis] = row_of(charges * sites[axis], eye)


def shards(
    equivariant_embedding,
    cartesian_coordinates,
    element_identity,
    occupied_site_totals,
    halo_export_indices,
    adjacency_rows,
    attention_source_weights,
    attention_target_weights,
    degree_channel_mixer,
    affinity_output_head,
    baseline_affinity_per_element,
    chemical_stiffness,
    reciprocal_lattice_points,
    ewald_weighting,
):
    chips_x = CHIPS_X
    ring = lax.axis_size("slab") // 2
    shape = (chips_x, ring, lax.axis_size("dom") // chips_x)
    assert shape[1] == shape[2]
    comps = equivariant_embedding.shape[3]
    ghosts = halo_export_indices.shape[2]
    blocks = reciprocal_lattice_points.shape[1] // LANES
    group = 2 * chips_x
    rows = 2 * blocks // group + SCALARS
    copies = 2 * (group - 1) + 2 * (ring - 1)
    table_size = LANES + 8 * ghosts
    bf16 = jnp.bfloat16
    vmem = pl.BlockSpec(memory_space=pltpu.VMEM)
    smem = pl.BlockSpec(memory_space=pltpu.SMEM)
    charges, forces = pl.pallas_call(
        lambda *refs: whole_kernel(shape, *refs),
        name="equilibrate",
        out_shape=(
            jax.ShapeDtypeStruct((1, LANES), F32),
            jax.ShapeDtypeStruct((3, 1, LANES), F32),
        ),
        in_specs=[vmem, vmem, vmem, smem, vmem, vmem, vmem, vmem, vmem, vmem, smem, smem, vmem, vmem],
        out_specs=(vmem, vmem),
        scratch_shapes=[
            pltpu.VMEM((LANES, LANES), bf16),
            pltpu.VMEM((comps + 1, LANES, LANES), bf16),
            pltpu.VMEM((comps + 1, ghosts, LANES), bf16),
            pltpu.VMEM((comps + 1, 8, ghosts, LANES), bf16),
            pltpu.VMEM((table_size, LANES), F32),
            pltpu.VMEM((LANES, table_size), F32),
            pltpu.VMEM((comps, LANES, LANES), F32),
            pltpu.VMEM((blocks, LANES, LANES), F32),
            pltpu.VMEM((blocks, LANES, LANES), F32),
            pltpu.VMEM((3, LANES, LANES), F32),
            pltpu.VMEM((5, LANES, LANES), F32),
            pltpu.VMEM((group, rows, LANES), F32),
            pltpu.VMEM((3, rows, LANES), F32),
            pltpu.VMEM((ITERS, copies - group + 1, rows, LANES), F32),
            pltpu.VMEM((ITERS, group, rows, LANES), F32),
            pltpu.VMEM((4, blocks, LANES), F32),
            pltpu.VMEM((2, blocks, LANES), F32),
            pltpu.SemaphoreType.DMA((8 * CHUNKS,)),
            pltpu.SemaphoreType.DMA((8 * CHUNKS,)),
            pltpu.SemaphoreType.DMA((copies,)),
            pltpu.SemaphoreType.DMA((ITERS, copies)),
        ],
        compiler_params=pltpu.CompilerParams(
            collective_id=1, has_side_effects=True, vmem_limit_bytes=48 * 1024 * 1024
        ),
    )(
        jnp.transpose(equivariant_embedding[0, 0], (1, 0, 2)),
        cartesian_coordinates[0, 0].reshape(3, 1, LANES),
        element_identity[0],
        occupied_site_totals,
        halo_export_indices[0],
        adjacency_rows[0, 0].T,
        attention_source_weights,
        attention_target_weights,
        degree_channel_mixer,
        affinity_output_head,
        baseline_affinity_per_element,
        chemical_stiffness,
        reciprocal_lattice_points,
        ewald_weighting.reshape(blocks, LANES),
    )
    return (charges.reshape(1, 1, LANES), forces.reshape(1, 1, 3, LANES))


def solution(mesh):
    placed = (
        P("dom", "slab", None, None, None),
        P("dom", "slab", None, None),
        P("dom", "slab", None),
        P("dom", "slab"),
        P("dom", "slab", None),
        P("dom", "slab", None, None),
        P(),
        P(),
        P(),
        P(),
        P(),
        P(),
        P(),
        P(),
    )
    return jax.shard_map(
        shards,
        mesh=mesh,
        in_specs=placed,
        out_specs=(P("dom", "slab", None), P("dom", "slab", None, None)),
        check_vma=False,
    )
```

time: 135 us -> 110 us (0.81)
  starting transfers between devices: 18.3 us -> 0 us
  Pallas kernels: 83.9 us -> 101 us
  matrix products: 10.2 us -> 0 us
  waiting for transfers between devices: 9.76 us -> 0 us
  other arithmetic: 8.13 us -> 0 us
  local copies, waits for them, and re-layouts: 2.8 us -> 7.65 us
    ppermute x4 -> x0, starting transfers between devices: 18.3 us -> none  [the longest x2 10.8 us: extended(): lax.ppermute(head, axis, [((i + 1) % count, i) for i in range(count)])]
    pallas_call x1, Pallas kernels: 83.9 us -> 101 us  [shards(): pl.pallas_call(lambda *refs: whole_kernel(shape, *refs), name='equilibrat...]
    dot_general x8 -> x0, matrix products: 10.2 us -> none  [the longest x5 5.78 us: project_values(): jnp.einsum('ncd,de->nce', row_block[:, first_comp:last_comp, :], degree_c...]
    ppermute x4 -> x0, waiting for transfers between devices: 9.76 us -> none  [the longest x2 6.38 us: extended(): lax.ppermute(tail, axis, [(i, (i + 1) % count) for i in range(count)])]
    unnamed x24 -> x28, local copies, waits for them, and re-layouts: 1.15 us -> 7.65 us
    reduce_sum x8 -> x0, other arithmetic: 5.45 us -> none  [the longest x4 4.19 us: readout_sum(): channel_norm = jnp.sqrt(jnp.sum(part_sq, axis=1) + 1e-06)]
    reduce_or x1 -> x0, other arithmetic: 2.31 us -> none  [shards(): jnp.any(neigh_dev[:, :, None] == columns[None, None, :], axis=1)]
  transfers between devices with their start and end apart: 4 -> 0, of which waited for: 4 -> 0; matrix products, arithmetic and copies ran while one was open for 2% -> 0% of each run, Pallas kernels for 0% -> 0%
where the time goes in v2:
time: 110 us
  Pallas kernels  101 us (92%)
  local copies, waits for them, and re-layouts  7.65 us (7%)
  between operations  1.35 us (1%)
    pallas_call x1, Pallas kernels, shards(): pl.pallas_call(lambda *refs: whole_kernel(shape, *refs), name='equilibrat...  101 us
    unnamed x28, local copies, waits for them, and re-layouts  7.65 us

profile of v2, /device:TPU:1, one launch (start us, length us, event | category | flops | bytes accessed | tf_op | source)
XLA Modules:
  0.0 109.8 jit_solution(11079404297204696977)
XLA Ops:
  1.3 0.0 copy-start.7
  1.3 0.0 copy-start.8
  1.3 0.0 copy-start.12
  1.3 0.0 copy-start.9
  1.3 0.0 copy-start.10
  1.3 0.0 copy-start.11
  1.3 0.6 copy-done.7
  2.0 0.0 copy-done.8
  2.0 0.0 copy-done.12
  2.0 0.0 copy-done.9
  2.0 0.0 copy-done.10
  2.0 0.0 copy-done.11
  2.0 0.0 copy-start
  2.0 1.1 %copy-done = bf16[1,1,128,25,128]{4,2,3,1,0:T(8,128)(2,1)S(1)} copy-done((bf16[1,1,128,25,128]{4,2,3,1,0:T(8,128)(2,1)S(1)}, bf16[1,1,128,25,128]{4,2,3,1,0:T(8,128)(2,1)}, u32[]{:S(2)}) %copy-start) | copy-done | bytes 819224
  3.2 0.0 copy-start.1
  3.2 0.9 copy-done.1
  4.1 0.0 copy-start.2
  4.1 0.8 copy-done.2
  4.9 0.0 copy-start.3
  4.9 0.8 copy-done.3
  5.7 0.0 copy-start.4
  5.7 0.8 copy-done.4
  6.4 0.0 copy-start.5
  6.4 0.8 copy-done.5
  7.2 0.0 copy-start.6
  7.2 0.7 copy-done.6
  7.9 100.9 %equilibrate.1 = (f32[1,128]{1,0:T(1,128)S(1)}, f32[3,1,128]{2,1,0:T(1,128)S(1)}) custom-call(bf16[25,128,128]{2,1,0:T(8,128)(2,1)S(1)} %bitcast.14, f32[3,1,128]{2,1,0:T(1,128)S(1)} %bitcast.17, s32[1,128]{1,0:T(1,128)S(1)} %bitcast.19, s32[1,1]{1,0:T(1,128)S(6)} %copy.19.refs_3_, s32[1,32]{1,0:T(1,128)S(1)} %bitcast.20, s32[64,128]{1,0:T(8,128)S(1)} %bitcast.15, ...), custom_call_target="tpu_custom_call" | custom-call | tf_op jit(solution)/shard_map/equilibrate/pallas_call | solution.py:483
  108.8 0.5 copy.20
  109.3 0.6 copy.21
Async XLA Ops:
  1.3 0.7 copy-start.7
  1.3 0.7 copy-start.8
  1.3 0.7 copy-start.12
  1.3 0.7 copy-start.9
  1.3 0.7 copy-start.10
  1.3 0.7 copy-start.11
  2.0 1.1 %copy-start = (bf16[1,1,128,25,128]{4,2,3,1,0:T(8,128)(2,1)S(1)}, bf16[1,1,128,25,128]{4,2,3,1,0:T(8,128)(2,1)}, u32[]{:S(2)}) copy-start(bf16[1,1,128,25,128]{4,2,3,1,0:T(8,128)(2,1)} %param.14) | copy-start | bytes 2457604
  3.2 0.9 copy-start.1
  4.1 0.8 copy-start.2
  4.9 0.8 copy-start.3
  5.7 0.8 copy-start.4
  6.4 0.8 copy-start.5
  7.2 0.7 copy-start.6

commit v3 on v2

v3 whole, which is shorter than its diff:
```python
import math

import jax
import jax.numpy as jnp
from jax import lax
from jax.experimental import pallas as pl
from jax.experimental.pallas import tpu as pltpu
from jax.sharding import PartitionSpec as P

ITERS = 4
CHIPS_X = 4
LANES = 128
MESH = pl.DeviceIdType.MESH
F32 = jnp.float32

HALF_PI_PARTS = (1.5703125, 4.837512969970703125e-4, 7.54978995489188216e-8)


def sine_cosine(phase):
    quadrant = jnp.round(phase * (2.0 / math.pi))
    reduced = phase - quadrant * HALF_PI_PARTS[0]
    reduced = reduced - quadrant * HALF_PI_PARTS[1]
    reduced = reduced - quadrant * HALF_PI_PARTS[2]
    square = reduced * reduced
    odd = (-1.9515295891e-4 * square + 8.3321608736e-3) * square - 1.6666654611e-1
    odd = odd * square * reduced + reduced
    even = (2.443315711809948e-5 * square - 1.388731625493765e-3) * square
    even = (even + 4.166664568298827e-2) * square * square - 0.5 * square + 1.0
    turn = quadrant.astype(jnp.int32)
    swap = (turn & 1) == 1
    sine = jnp.where(swap, even, odd)
    cosine = jnp.where(swap, odd, even)
    sine = jnp.where((turn & 2) == 2, -sine, sine)
    cosine = jnp.where(((turn + 1) & 2) == 2, -cosine, cosine)
    return sine, cosine


CHUNKS = 2
SCALARS = 3
TILE = 8


def place_of(shape):
    chips_x, chips_y, chips_z = shape
    dom, slab = lax.axis_index("dom"), lax.axis_index("slab")
    return dom // chips_z, slab // 2, dom % chips_z, slab % 2


def device(shape, x, y, z, core):
    return (x * shape[2] + z, y * 2 + core)


def far_first(count):
    return sorted(range(1, count), key=lambda j: -min(j, count - j))


def sum_partners(shape):
    x, y, z, core = place_of(shape)
    chips_x, ring, _ = shape
    group = 2 * chips_x
    mine = x * 2 + core
    peers = []
    for i in far_first(group):
        other = (mine + i) % group
        peers.append((other, device(shape, other // 2, y, z, other % 2)))
    along = [
        device(shape, x, (y + j * (1 - core)) % ring, (z + j * core) % ring, core)
        for j in far_first(ring)
    ]
    across = [
        device(shape, x, (y + j * core) % ring, (z + j * (1 - core)) % ring, core)
        for j in far_first(ring)
    ]
    return mine, peers, along, across


def halo_partners(shape):
    x, y, z, core = place_of(shape)
    domains = shape[0] * shape[2]
    dom, slab = lax.axis_index("dom"), lax.axis_index("slab")
    way = 1 - 2 * core
    return {
        "before": ((dom + domains - 1) % domains, slab),
        "after": ((dom + 1) % domains, slab),
        "pair": (dom, y * 2 + 1 - core),
        "outer": (dom, (slab + 2 * shape[1] - way) % (2 * shape[1])),
        "ahead": ((dom + domains + way) % domains, slab),
    }


def row_of(column, eye):
    return jnp.sum(jnp.where(eye, column, 0.0), axis=0, keepdims=True)


def identity_mask(count):
    shape = (count, count)
    return lax.broadcasted_iota(jnp.int32, shape, 0) == lax.broadcasted_iota(jnp.int32, shape, 1)


def degrees_of(comps):
    return [range(l * l, (l + 1) * (l + 1)) for l in range(math.isqrt(comps))]


def fill_mask(adjacency_ref, upright, mask_ref):
    size = upright.shape[0]
    ghosts = (size - LANES) // 8
    group = 64

    def per_group(part, carry):
        start = part * group
        row = lax.broadcasted_iota(jnp.int32, (group, LANES), 0) + start
        row = row + jnp.where(row >= LANES + 4 * ghosts, ghosts, 0)
        hit = row == adjacency_ref[0:1, :]
        for j in range(1, adjacency_ref.shape[0]):
            hit = hit | (row == adjacency_ref[j : j + 1, :])
        upright[pl.ds(pl.multiple_of(start, group), group), :] = jnp.where(hit, 1.0, 0.0)
        return carry

    lax.fori_loop(0, size // group, per_group, 0)
    for part in range(size // LANES):
        span = slice(part * LANES, (part + 1) * LANES)
        mask_ref[:, span] = upright[span, :].T


def attention(queries, keys, mask):
    scores = lax.dot_general(
        queries, keys, (((1,), (1,)), ((), ())), preferred_element_type=F32
    )
    gate = jax.nn.sigmoid(scores / math.sqrt(LANES)) * 0.125
    return jnp.where(mask > 0.0, gate, 0.0).astype(jnp.bfloat16)


def spread(rows):
    return jnp.concatenate([rows] * (LANES // rows.shape[0]), axis=0).T


def wide(columns, index):
    return jnp.broadcast_to(columns[:, index : index + 1], (LANES, LANES))


def fill_tables(first, stop, blocks, waves, about, sites, cos_ref, sin_ref):
    step_rows = 64

    def per_member(member, carry):
        columns = spread(about[member])
        for axis in range(3):
            sites[axis] = wide(columns, axis)

        def per_rows(part, inner):
            block, rows = part // (LANES // step_rows), part % (LANES // step_rows)
            lanes = pl.ds(pl.multiple_of(block * LANES, LANES), LANES)
            rows = pl.ds(pl.multiple_of(rows * step_rows, step_rows), step_rows)
            phase = (
                sites[0, rows, :] * waves[0:1, lanes]
                + sites[1, rows, :] * waves[1:2, lanes]
                + sites[2, rows, :] * waves[2:3, lanes]
            )
            sine, cosine = sine_cosine(phase)
            cos_ref[member * blocks + block, rows, :] = cosine
            sin_ref[member * blocks + block, rows, :] = sine
            return inner

        return lax.fori_loop(0, blocks * LANES // step_rows, per_rows, carry)

    lax.fori_loop(first, stop, per_member, 0)


def whole_kernel(
    shape,
    features_hbm,
    mixer_hbm,
    source_hbm,
    target_hbm,
    export_hbm,
    place_hbm,
    species_hbm,
    adjacency_hbm,
    head_hbm,
    weight_hbm,
    waves_hbm,
    count_ref,
    baseline_ref,
    stiffness_ref,
    charges_ref,
    forces_ref,
    features_ref,
    mixer_ref,
    source_ref,
    target_ref,
    export_ref,
    place_ref,
    species_ref,
    adjacency_ref,
    head_ref,
    weight_ref,
    waves,
    queries,
    table,
    outgoing,
    arrived,
    upright,
    mask_ref,
    own_message,
    cos_ref,
    sin_ref,
    sites,
    about,
    first_rows,
    vectors,
    parts,
    inbox,
    ring_total,
    factors,
    posts,
    post_inbox,
    post_total,
    matrix,
    fields,
    field_inbox,
    load_sem,
    halo_send,
    halo_recv,
    near_recv,
    group_send,
    group_recv,
    ring_send,
    ring_recv,
):
    me, peers, along, across = sum_partners(shape)
    near = halo_partners(shape)
    core = place_of(shape)[3]
    group = len(peers) + 1
    everyone = [peer for _, peer in peers] + along + across
    everyone += [near[name] for name in ("before", "after", "pair", "outer")]
    barrier = pltpu.get_barrier_semaphore()
    for partner in everyone:
        pl.semaphore_signal(barrier, inc=1, device_id=partner, device_id_type=MESH)

    comps = features_ref.shape[0]
    ghosts = outgoing.shape[1]
    blocks = cos_ref.shape[0] // group
    span = blocks * LANES
    scale = 1.0 / math.sqrt(lax.axis_size("dom") * lax.axis_size("slab") * LANES)
    bf16 = jnp.bfloat16

    own_waves = waves_hbm.at[:, pl.ds(pl.multiple_of(me * span, LANES), span)]
    loads = [
        pltpu.make_async_copy(source, target, load_sem.at[i])
        for i, (source, target) in enumerate(
            (
                (features_hbm, features_ref),
                (mixer_hbm, mixer_ref),
                (source_hbm, source_ref),
                (target_hbm, target_ref),
                (export_hbm, export_ref),
                (place_hbm, place_ref),
                (species_hbm, species_ref),
                (adjacency_hbm, adjacency_ref),
                (head_hbm, head_ref),
                (weight_hbm, weight_ref),
                (own_waves, waves),
            )
        )
    ]
    for item in loads:
        item.start()
    eye = identity_mask(LANES)

    loads[5].wait()
    loads[6].wait()
    species = species_ref[...]
    hardness = jnp.zeros(species.shape, F32)
    baseline = jnp.zeros(species.shape, F32)
    for element in range(stiffness_ref.shape[0]):
        hardness = jnp.where(species == element, stiffness_ref[element], hardness)
        baseline = jnp.where(species == element, baseline_ref[element], baseline)
    live = lax.broadcasted_iota(jnp.int32, (1, LANES), 1) < count_ref[0, 0]
    live = jnp.where(live, 1.0, 0.0)
    about[me] = jnp.zeros((TILE, LANES), F32)
    for axis in range(3):
        about[me, axis : axis + 1, :] = place_ref[axis]
    about[me, 3:4, :] = hardness
    about[me, 4:5, :] = live

    for i in range(5):
        loads[i].wait()
    for degree, members in enumerate(degrees_of(comps)):
        for comp in members:
            product = jnp.dot(
                features_ref[comp], mixer_ref[degree], preferred_element_type=F32
            )
            table[comp] = product.astype(bf16)
    scalar = features_ref[0]
    table[comps] = jnp.dot(scalar, target_ref[...], preferred_element_type=F32).astype(bf16)
    queries[...] = jnp.dot(scalar, source_ref[...], preferred_element_type=F32).astype(bf16)
    offered = jnp.broadcast_to(export_ref[...], (ghosts, ghosts)).astype(F32)
    offered = jnp.sum(jnp.where(identity_mask(ghosts), offered, 0.0), axis=1, keepdims=True)
    slots = lax.broadcasted_iota(jnp.int32, (ghosts, LANES), 1).astype(F32)
    pick = jnp.where(slots == offered, 1.0, 0.0).astype(bf16)
    for comp in range(comps + 1):
        row = jnp.dot(pick, table[comp], preferred_element_type=F32)
        outgoing[comp] = row.astype(bf16)

    pl.semaphore_wait(barrier, len(everyone))

    size = (comps + 1) // CHUNKS

    def ship(chunk, source, slot, target, sem):
        rows = pl.ds(chunk * size, size)
        copy = pltpu.make_async_remote_copy(
            src_ref=source,
            dst_ref=arrived.at[rows, slot],
            send_sem=halo_send,
            recv_sem=sem,
            device_id=target,
            device_id_type=MESH,
        )
        copy.start()

    def own(chunk):
        return outgoing.at[pl.ds(chunk * size, size)]

    def got(chunk, slot):
        return arrived.at[pl.ds(chunk * size, size), slot]

    def all_of(ref, send, receive):
        return pltpu.make_async_remote_copy(
            src_ref=ref,
            dst_ref=ref,
            send_sem=send,
            recv_sem=receive,
            device_id=near["pair"],
            device_id_type=MESH,
        )

    def to_group(pieces, drops, stage):
        for i, (_, target) in enumerate(peers):
            pltpu.make_async_remote_copy(
                src_ref=pieces(i),
                dst_ref=drops(i),
                send_sem=group_send.at[stage],
                recv_sem=group_recv.at[stage],
                device_id=target,
                device_id_type=MESH,
            ).start()

    for chunk in range(CHUNKS):
        ship(chunk, own(chunk), 1, near["after"], near_recv.at[chunk, 0])
        ship(chunk, own(chunk), 6, near["before"], near_recv.at[chunk, 0])
        ship(chunk, own(chunk), 4 - core, near["outer"], near_recv.at[chunk, 1])
        ship(chunk, own(chunk), 3 + core, near["pair"], halo_recv)
        if chunk == 0:
            to_group(lambda i: about.at[me], lambda i: about.at[me], 0)

    loads[7].wait()
    fill_mask(adjacency_ref, upright, mask_ref)
    own_weights = attention(queries[...], table[comps], mask_ref[:, 0:LANES])
    for comp in range(comps):
        own_message[comp] = jnp.dot(own_weights, table[comp], preferred_element_type=F32)

    for i in range(8, 11):
        loads[i].wait()
    others = about.at[pl.ds(0, group - 1)]
    all_of(others, group_send.at[0], group_recv.at[0]).wait_recv()
    for chunk in range(CHUNKS):
        fill_tables(
            chunk * group // CHUNKS,
            (chunk + 1) * group // CHUNKS,
            blocks,
            waves,
            about,
            sites,
            cos_ref,
            sin_ref,
        )
        all_of(got(chunk, 0), halo_send, near_recv.at[chunk, 1]).wait_recv()
        ship(chunk, got(chunk, 3 + core), 7 * core, near["ahead"], halo_recv)
        both = arrived.at[pl.ds(chunk * size, size), pl.ds(0, 2)]
        all_of(both, halo_send, near_recv.at[chunk, 0]).wait_recv()
        ship(chunk, got(chunk, 1 + 5 * core), 2 + 3 * core, near["outer"], halo_recv)
        ship(chunk, got(chunk, 1), 2 * core, near["pair"], halo_recv)
        ship(chunk, got(chunk, 6), 5 + 2 * core, near["pair"], halo_recv)
    for member in range(group):
        vectors[3, member : member + 1, :] = about[member, 3:4, :]
        vectors[4, member : member + 1, :] = about[member, 4:5, :]
    vectors[1] = jnp.zeros((group, LANES), F32)
    vectors[2] = jnp.zeros((group, LANES), F32)
    factors[...] = jnp.zeros_like(factors)
    all_of(arrived.at[:, pl.ds(0, 5)], halo_send, halo_recv).wait_recv()

    ghost_keys = arrived[comps].reshape(8 * ghosts, LANES)
    weights = attention(queries[...], ghost_keys, mask_ref[:, LANES:])
    readout = jnp.zeros((LANES, LANES), F32)
    for degree, members in enumerate(degrees_of(comps)):
        square = jnp.zeros((LANES, LANES), F32)
        for comp in members:
            message = own_message[comp] + jnp.dot(
                weights, arrived[comp].reshape(8 * ghosts, LANES), preferred_element_type=F32
            )
            square = message if degree == 0 else square + message * message
        norm = square if degree == 0 else jnp.sqrt(square + 1e-06)
        readout = readout + norm * head_ref[degree : degree + 1, :]
    electroneg = row_of(jnp.sum(readout, axis=1, keepdims=True), eye) + baseline
    first_rows[me] = -electroneg * live
    to_group(lambda i: first_rows.at[me], lambda i: first_rows.at[me], 1)
    all_of(arrived, halo_send, halo_recv).wait_send()
    all_of(others, group_send.at[0], group_recv.at[0]).wait_send()
    starts = first_rows.at[pl.ds(0, group - 1)]
    all_of(starts, group_send.at[1], group_recv.at[1]).wait()
    for member in range(group):
        vectors[0, member : member + 1, :] = first_rows[member]

    lanes = lax.broadcasted_iota(jnp.int32, (LANES, LANES), 1)
    scalar_row = 2 * blocks
    weight = weight_ref[me]
    tables = (cos_ref, sin_ref)

    def full_sum(rows):
        return jnp.sum(jnp.sum(rows, axis=0, keepdims=True), axis=1, keepdims=True)

    def project(turn):
        residual = vectors[0]
        columns = spread(residual)
        sums = [[jnp.zeros((TILE, LANES), F32) for _ in range(blocks)] for _ in range(2)]
        for member in range(group):
            column = wide(columns, member)
            for part in range(2):
                for block in range(blocks):
                    product = tables[part][member * blocks + block] * column
                    product = product.reshape(LANES // TILE, TILE, LANES)
                    sums[part][block] = sums[part][block] + jnp.sum(product, axis=0)
        for part in range(2):
            for block in range(blocks):
                row = part * blocks + block
                parts[turn, 0, row : row + 1, :] = jnp.sum(
                    sums[part][block], axis=0, keepdims=True
                )
        hard_residual = vectors[3] * residual
        scalars = (residual * residual, hard_residual * residual, hard_residual * vectors[1])
        for i, product in enumerate(scalars):
            row = scalar_row + i
            parts[turn, 0, row : row + 1, :] = jnp.broadcast_to(full_sum(product), (1, LANES))

    def ring_sum(turn, meanwhile):
        held = parts[turn, 0]
        for stage, targets in enumerate((along, across)):
            if stage > 0:
                parts[turn, stage] = held
            for i, target in enumerate(targets):
                pltpu.make_async_remote_copy(
                    src_ref=parts.at[turn, stage],
                    dst_ref=inbox.at[turn, stage, i],
                    send_sem=ring_send.at[stage],
                    recv_sem=ring_recv.at[turn, stage],
                    device_id=target,
                    device_id_type=MESH,
                ).start()
            if stage == 0:
                meanwhile()
            all_of(inbox.at[turn, stage], ring_send.at[stage], ring_recv.at[turn, stage]).wait()
            for i in range(len(targets)):
                held = held + inbox[turn, stage, i]
        ring_total[...] = held

    def follow(turn, previous_norm, stiff_part):
        norm, pure, mixed = (
            ring_total[scalar_row + i : scalar_row + i + 1, :] for i in range(SCALARS)
        )
        beta = jnp.where(turn > 0, norm / previous_norm, 0.0)
        stiff_part = pure + 2.0 * beta * mixed + beta * beta * stiff_part
        recip = jnp.zeros_like(weight)
        for part in range(2):
            rows = ring_total[part * blocks : (part + 1) * blocks, :] + beta * factors[part]
            factors[part] = rows
            factors[2 + part] = weight * rows
            recip = recip + weight * rows * rows
        vectors[1] = vectors[0] + beta * vectors[1]
        return norm, stiff_part, jnp.broadcast_to(full_sum(recip), (1, LANES))

    def iteration(turn, carry):
        project(turn)
        ring_sum(turn, lambda: None)
        norm, stiff_part, recip = follow(turn, *carry)

        def back(member, acc):
            image = jnp.zeros((LANES, LANES), F32)
            for block in range(blocks):
                for part in range(2):
                    row = factors[2 + part, block : block + 1, :]
                    image = image + tables[part][member * blocks + block] * row
            return jnp.where(lanes == member, jnp.sum(image, axis=1, keepdims=True), acc)

        images = lax.fori_loop(0, group, back, jnp.zeros((LANES, LANES), F32))
        posts[turn, 0:group, :] = images.T[0:group, :]
        posts[turn, group : group + 1, :] = recip
        to_group(lambda i: posts.at[turn], lambda i: post_inbox.at[turn, i], 2 + turn)
        held = posts[turn]
        all_of(post_inbox.at[turn], group_send.at[2 + turn], group_recv.at[2 + turn]).wait()
        for i in range(group - 1):
            held = held + post_inbox[turn, i]
        post_total[...] = held
        step = norm / (stiff_part + scale * post_total[group : group + 1, :])
        direction = vectors[1]
        image = vectors[4] * (vectors[3] * direction + scale * post_total[0:group, :])
        vectors[2] = vectors[2] + step * direction
        vectors[0] = vectors[0] - step * image
        for part in range(2):
            factors[4 + part] = factors[4 + part] + step * factors[2 + part]
        return norm, stiff_part

    def field_of(first, offset):
        half = LANES // 2

        def per_member(member, carry):
            for part in range(2):
                rows = pl.ds(part * half, half)
                sums = [jnp.zeros((half, LANES), F32) for _ in range(3)]
                for block in range(blocks):
                    where = member * blocks + block
                    term = (
                        sin_ref[where, rows, :] * factors[first, block : block + 1, :]
                        - cos_ref[where, rows, :] * factors[first + 1, block : block + 1, :]
                    )
                    for axis in range(3):
                        wave = waves[axis : axis + 1, block * LANES : (block + 1) * LANES]
                        sums[axis] = sums[axis] + term * wave
                filled = matrix[rows, :]
                for axis in range(3):
                    column = jnp.sum(sums[axis], axis=1, keepdims=True)
                    place = member * TILE + offset + axis
                    filled = jnp.where(lanes[0:half, :] == place, column, filled)
                matrix[rows, :] = filled
            return carry

        lax.fori_loop(0, group, per_member, 0)

    ones = jnp.ones((1, LANES), F32)
    carry = lax.fori_loop(0, ITERS - 1, iteration, (ones, ones))

    turn = ITERS - 1
    matrix[...] = jnp.zeros_like(matrix)
    project(turn)
    ring_sum(turn, lambda: field_of(4, 0))
    norm, stiff_part, recip = follow(turn, *carry)
    field_of(2, 3)
    field_rows = matrix[...].T
    for member in range(group):
        fields[member] = field_rows[member * TILE : (member + 1) * TILE, :]
        fields[member, 6:7, :] = recip
    stage = 1 + ITERS
    to_group(lambda i: fields.at[peers[i][0]], lambda i: field_inbox.at[i], stage)
    held = fields[me]
    all_of(field_inbox, group_send.at[stage], group_recv.at[stage]).wait()
    for i in range(group - 1):
        held = held + field_inbox[i]
    fields[me] = held
    step = norm / (stiff_part + scale * fields[me, 6:7, :])
    vectors[2] = vectors[2] + step * vectors[1]
    charges = vectors[2, pl.ds(me, 1), :]
    charges_ref[...] = charges
    for axis in range(3):
        field = fields[me, axis : axis + 1, :] + step * fields[me, 3 + axis : 4 + axis, :]
        forces_ref[axis] = charges * (scale * field)


def shards(
    equivariant_embedding,
    cartesian_coordinates,
    element_identity,
    occupied_site_totals,
    halo_export_indices,
    adjacency_rows,
    attention_source_weights,
    attention_target_weights,
    degree_channel_mixer,
    affinity_output_head,
    baseline_affinity_per_element,
    chemical_stiffness,
    reciprocal_lattice_points,
    ewald_weighting,
):
    chips_x = CHIPS_X
    ring = lax.axis_size("slab") // 2
    shape = (chips_x, ring, lax.axis_size("dom") // chips_x)
    assert shape[1] == shape[2]
    comps = equivariant_embedding.shape[3]
    ghosts = halo_export_indices.shape[2]
    degrees = degree_channel_mixer.shape[0]
    lists = adjacency_rows.shape[3]
    group = 2 * chips_x
    blocks = reciprocal_lattice_points.shape[1] // LANES // group
    rows = 2 * blocks + SCALARS
    table_size = LANES + 8 * ghosts
    bf16, i32 = jnp.bfloat16, jnp.int32
    assert group * TILE <= LANES and (comps + 1) % CHUNKS == 0
    vmem = pl.BlockSpec(memory_space=pltpu.VMEM)
    smem = pl.BlockSpec(memory_space=pltpu.SMEM)
    hbm = pl.BlockSpec(memory_space=pltpu.HBM)
    dma = pltpu.SemaphoreType.DMA
    charges, forces = pl.pallas_call(
        lambda *refs: whole_kernel(shape, *refs),
        name="equilibrate",
        out_shape=(
            jax.ShapeDtypeStruct((1, LANES), F32),
            jax.ShapeDtypeStruct((3, 1, LANES), F32),
        ),
        in_specs=[hbm] * 11 + [smem] * 3,
        out_specs=(vmem, vmem),
        scratch_shapes=[
            pltpu.VMEM((comps, LANES, LANES), bf16),
            pltpu.VMEM((degrees, LANES, LANES), bf16),
            pltpu.VMEM((LANES, LANES), bf16),
            pltpu.VMEM((LANES, LANES), bf16),
            pltpu.VMEM((1, ghosts), i32),
            pltpu.VMEM((3, 1, LANES), F32),
            pltpu.VMEM((1, LANES), i32),
            pltpu.VMEM((lists, LANES), i32),
            pltpu.VMEM((degrees, LANES), F32),
            pltpu.VMEM((group, blocks, LANES), F32),
            pltpu.VMEM((3, blocks * LANES), F32),
            pltpu.VMEM((LANES, LANES), bf16),
            pltpu.VMEM((comps + 1, LANES, LANES), bf16),
            pltpu.VMEM((comps + 1, ghosts, LANES), bf16),
            pltpu.VMEM((comps + 1, 8, ghosts, LANES), bf16),
            pltpu.VMEM((table_size, LANES), F32),
            pltpu.VMEM((LANES, table_size), F32),
            pltpu.VMEM((comps, LANES, LANES), F32),
            pltpu.VMEM((group * blocks, LANES, LANES), F32),
            pltpu.VMEM((group * blocks, LANES, LANES), F32),
            pltpu.VMEM((3, LANES, LANES), F32),
            pltpu.VMEM((group, TILE, LANES), F32),
            pltpu.VMEM((group, 1, LANES), F32),
            pltpu.VMEM((5, group, LANES), F32),
            pltpu.VMEM((ITERS, 2, rows, LANES), F32),
            pltpu.VMEM((ITERS, 2, ring - 1, rows, LANES), F32),
            pltpu.VMEM((rows, LANES), F32),
            pltpu.VMEM((6, blocks, LANES), F32),
            pltpu.VMEM((ITERS - 1, group + 1, LANES), F32),
            pltpu.VMEM((ITERS - 1, group - 1, group + 1, LANES), F32),
            pltpu.VMEM((group + 1, LANES), F32),
            pltpu.VMEM((LANES, LANES), F32),
            pltpu.VMEM((group, TILE, LANES), F32),
            pltpu.VMEM((group - 1, TILE, LANES), F32),
            dma((11,)),
            dma,
            dma,
            dma((CHUNKS, 2)),
            dma((ITERS + 2,)),
            dma((ITERS + 2,)),
            dma((2,)),
            dma((ITERS, 2)),
        ],
        compiler_params=pltpu.CompilerParams(
            collective_id=1, has_side_effects=True, vmem_limit_bytes=48 * 1024 * 1024
        ),
    )(
        jnp.transpose(equivariant_embedding[0, 0], (1, 0, 2)),
        degree_channel_mixer,
        attention_source_weights,
        attention_target_weights,
        halo_export_indices[0],
        cartesian_coordinates[0, 0].reshape(3, 1, LANES),
        element_identity[0],
        adjacency_rows[0, 0].T,
        affinity_output_head,
        ewald_weighting.reshape(group, blocks, LANES),
        reciprocal_lattice_points,
        occupied_site_totals,
        baseline_affinity_per_element,
        chemical_stiffness,
    )
    return (charges.reshape(1, 1, LANES), forces.reshape(1, 1, 3, LANES))


def solution(mesh):
    placed = (
        P("dom", "slab", None, None, None),
        P("dom", "slab", None, None),
        P("dom", "slab", None),
        P("dom", "slab"),
        P("dom", "slab", None),
        P("dom", "slab", None, None),
        P(),
        P(),
        P(),
        P(),
        P(),
        P(),
        P(),
        P(),
    )
    return jax.shard_map(
        shards,
        mesh=mesh,
        in_specs=placed,
        out_specs=(P("dom", "slab", None), P("dom", "slab", None, None)),
        check_vma=False,
    )
```

time: 110 us -> 104 us (0.945)
  Pallas kernels: 101 us -> 94.6 us
    pallas_call x1, Pallas kernels: 101 us -> 94.6 us  [shards(): pl.pallas_call(lambda *refs: whole_kernel(shape, *refs), name='equilibrat...]
where the time goes in v3:
time: 104 us
  Pallas kernels  94.6 us (91%)
  local copies, waits for them, and re-layouts  7.65 us (7%)
  between operations  1.35 us (1%)
    pallas_call x1, Pallas kernels, shards(): pl.pallas_call(lambda *refs: whole_kernel(shape, *refs), name='equilibrat...  94.6 us
    unnamed x28, local copies, waits for them, and re-layouts  7.65 us

profile of v3, /device:TPU:1, one launch (start us, length us, event | category | flops | bytes accessed | tf_op | source)
XLA Modules:
  0.0 103.6 jit_solution(9949959394599348380)
XLA Ops:
  1.3 0.0 copy-start.7
  1.3 0.0 copy-start.8
  1.3 0.0 copy-start.12
  1.3 0.0 copy-start.9
  1.3 0.0 copy-start.10
  1.3 0.0 copy-start.11
  1.3 0.6 copy-done.7
  2.0 0.0 copy-done.8
  2.0 0.0 copy-done.12
  2.0 0.0 copy-done.9
  2.0 0.0 copy-done.10
  2.0 0.0 copy-done.11
  2.0 0.0 copy-start
  2.0 1.1 %copy-done = bf16[1,1,128,25,128]{4,2,3,1,0:T(8,128)(2,1)S(1)} copy-done((bf16[1,1,128,25,128]{4,2,3,1,0:T(8,128)(2,1)S(1)}, bf16[1,1,128,25,128]{4,2,3,1,0:T(8,128)(2,1)}, u32[]{:S(2)}) %copy-start) | copy-done | bytes 819224
  3.2 0.0 copy-start.1
  3.2 0.9 copy-done.1
  4.1 0.0 copy-start.2
  4.1 0.8 copy-done.2
  4.9 0.0 copy-start.3
  4.9 0.8 copy-done.3
  5.7 0.0 copy-start.4
  5.7 0.8 copy-done.4
  6.4 0.0 copy-start.5
  6.4 0.8 copy-done.5
  7.2 0.0 copy-start.6
  7.2 0.7 copy-done.6
  7.9 94.6 %equilibrate.1 = (f32[1,128]{1,0:T(1,128)S(1)}, f32[3,1,128]{2,1,0:T(1,128)S(1)}) custom-call(bf16[25,128,128]{2,1,0:T(8,128)(2,1)S(1)} %bitcast.14, bf16[5,128,128]{2,1,0:T(8,128)(2,1)S(1)} %copy-done.1, bf16[128,128]{1,0:T(8,128)(2,1)S(1)} %copy-done.3, bf16[128,128]{1,0:T(8,128)(2,1)S(1)} %copy-done.4, s32[1,32]{1,0:T(1,128)S(1)} %bitcast.19, ...), custom_call_target="tpu_custom_call" | custom-call | tf_op jit(solution)/shard_map/equilibrate/pallas_call | solution.py:600
  102.5 0.5 copy.20
  103.1 0.6 copy.21
Async XLA Ops:
  1.3 0.7 copy-start.7
  1.3 0.7 copy-start.8
  1.3 0.7 copy-start.12
  1.3 0.7 copy-start.9
  1.3 0.7 copy-start.10
  1.3 0.7 copy-start.11
  2.0 1.1 %copy-start = (bf16[1,1,128,25,128]{4,2,3,1,0:T(8,128)(2,1)S(1)}, bf16[1,1,128,25,128]{4,2,3,1,0:T(8,128)(2,1)}, u32[]{:S(2)}) copy-start(bf16[1,1,128,25,128]{4,2,3,1,0:T(8,128)(2,1)} %param.14) | copy-start | bytes 2457604
  3.2 0.9 copy-start.1
  4.1 0.8 copy-start.2
  4.9 0.8 copy-start.3
  5.7 0.8 copy-start.4
  6.4 0.8 copy-start.5
  7.2 0.7 copy-start.6

commit v4 on v3

--- a/solution.py
+++ b/solution.py
@@ -36,6 +36,7 @@
 
 
 CHUNKS = 2
+BLOCKS = (1, 7, 3, 5, 0, 2, 6, 8)
 SCALARS = 3
 TILE = 8
 
@@ -43,7 +44,7 @@
 def place_of(shape):
     chips_x, chips_y, chips_z = shape
     dom, slab = lax.axis_index("dom"), lax.axis_index("slab")
-    return dom // chips_z, slab // 2, dom % chips_z, slab % 2
+    return lax.div(dom, chips_z), lax.div(slab, 2), lax.rem(dom, chips_z), lax.rem(slab, 2)
 
 
 def device(shape, x, y, z, core):
@@ -61,14 +62,14 @@
     mine = x * 2 + core
     peers = []
     for i in far_first(group):
-        other = (mine + i) % group
-        peers.append((other, device(shape, other // 2, y, z, other % 2)))
+        other = lax.rem(mine + i, group)
+        peers.append((other, device(shape, lax.div(other, 2), y, z, lax.rem(other, 2))))
     along = [
-        device(shape, x, (y + j * (1 - core)) % ring, (z + j * core) % ring, core)
+        device(shape, x, lax.rem(y + j * (1 - core), ring), lax.rem(z + j * core, ring), core)
         for j in far_first(ring)
     ]
     across = [
-        device(shape, x, (y + j * core) % ring, (z + j * (1 - core)) % ring, core)
+        device(shape, x, lax.rem(y + j * core, ring), lax.rem(z + j * (1 - core), ring), core)
         for j in far_first(ring)
     ]
     return mine, peers, along, across
@@ -80,11 +81,11 @@
     dom, slab = lax.axis_index("dom"), lax.axis_index("slab")
     way = 1 - 2 * core
     return {
-        "before": ((dom + domains - 1) % domains, slab),
-        "after": ((dom + 1) % domains, slab),
+        "before": (lax.rem(dom + domains - 1, domains), slab),
+        "after": (lax.rem(dom + 1, domains), slab),
         "pair": (dom, y * 2 + 1 - core),
-        "outer": (dom, (slab + 2 * shape[1] - way) % (2 * shape[1])),
-        "ahead": ((dom + domains + way) % domains, slab),
+        "outer": (dom, lax.rem(slab + 2 * shape[1] - way, 2 * shape[1])),
+        "ahead": (lax.rem(dom + domains + way, domains), slab),
     }
 
 
@@ -109,7 +110,12 @@
     def per_group(part, carry):
         start = part * group
         row = lax.broadcasted_iota(jnp.int32, (group, LANES), 0) + start
-        row = row + jnp.where(row >= LANES + 4 * ghosts, ghosts, 0)
+        slot = row - LANES
+        shift = jnp.zeros_like(row)
+        for i, block in enumerate(BLOCKS):
+            inside = (slot >= i * ghosts) & (slot < (i + 1) * ghosts)
+            shift = jnp.where(inside, (block - i) * ghosts, shift)
+        row = row + shift
         hit = row == adjacency_ref[0:1, :]
         for j in range(1, adjacency_ref.shape[0]):
             hit = hit | (row == adjacency_ref[j : j + 1, :])
@@ -178,9 +184,9 @@
     head_hbm,
     weight_hbm,
     waves_hbm,
+    baseline_hbm,
+    stiffness_hbm,
     count_ref,
-    baseline_ref,
-    stiffness_ref,
     charges_ref,
     forces_ref,
     features_ref,
@@ -194,6 +200,8 @@
     head_ref,
     weight_ref,
     waves,
+    baseline_ref,
+    stiffness_ref,
     queries,
     table,
     outgoing,
@@ -230,12 +238,6 @@
     near = halo_partners(shape)
     core = place_of(shape)[3]
     group = len(peers) + 1
-    everyone = [peer for _, peer in peers] + along + across
-    everyone += [near[name] for name in ("before", "after", "pair", "outer")]
-    barrier = pltpu.get_barrier_semaphore()
-    for partner in everyone:
-        pl.semaphore_signal(barrier, inc=1, device_id=partner, device_id_type=MESH)
-
     comps = features_ref.shape[0]
     ghosts = outgoing.shape[1]
     blocks = cos_ref.shape[0] // group
@@ -259,21 +261,29 @@
                 (head_hbm, head_ref),
                 (weight_hbm, weight_ref),
                 (own_waves, waves),
+                (baseline_hbm, baseline_ref),
+                (stiffness_hbm, stiffness_ref),
             )
         )
     ]
     for item in loads:
         item.start()
+    everyone = [near[name] for name in ("before", "after", "pair", "outer")]
+    everyone += [peer for _, peer in peers] + along + across
+    barrier = pltpu.get_barrier_semaphore()
+    for partner in everyone:
+        pl.semaphore_signal(barrier, inc=1, device_id=partner, device_id_type=MESH)
     eye = identity_mask(LANES)
 
-    loads[5].wait()
-    loads[6].wait()
+    for i in (5, 6, 11, 12):
+        loads[i].wait()
     species = species_ref[...]
     hardness = jnp.zeros(species.shape, F32)
     baseline = jnp.zeros(species.shape, F32)
-    for element in range(stiffness_ref.shape[0]):
-        hardness = jnp.where(species == element, stiffness_ref[element], hardness)
-        baseline = jnp.where(species == element, baseline_ref[element], baseline)
+    for element in range(stiffness_ref.shape[1]):
+        here = species == element
+        hardness = jnp.where(here, stiffness_ref[0:1, element : element + 1], hardness)
+        baseline = jnp.where(here, baseline_ref[0:1, element : element + 1], baseline)
     live = lax.broadcasted_iota(jnp.int32, (1, LANES), 1) < count_ref[0, 0]
     live = jnp.where(live, 1.0, 0.0)
     about[me] = jnp.zeros((TILE, LANES), F32)
@@ -284,26 +294,20 @@
 
     for i in range(5):
         loads[i].wait()
-    for degree, members in enumerate(degrees_of(comps)):
-        for comp in members:
-            product = jnp.dot(
-                features_ref[comp], mixer_ref[degree], preferred_element_type=F32
-            )
-            table[comp] = product.astype(bf16)
-    scalar = features_ref[0]
-    table[comps] = jnp.dot(scalar, target_ref[...], preferred_element_type=F32).astype(bf16)
-    queries[...] = jnp.dot(scalar, source_ref[...], preferred_element_type=F32).astype(bf16)
     offered = jnp.broadcast_to(export_ref[...], (ghosts, ghosts)).astype(F32)
     offered = jnp.sum(jnp.where(identity_mask(ghosts), offered, 0.0), axis=1, keepdims=True)
     slots = lax.broadcasted_iota(jnp.int32, (ghosts, LANES), 1).astype(F32)
     pick = jnp.where(slots == offered, 1.0, 0.0).astype(bf16)
-    for comp in range(comps + 1):
-        row = jnp.dot(pick, table[comp], preferred_element_type=F32)
-        outgoing[comp] = row.astype(bf16)
+    size = (comps + 1) // CHUNKS
+
+    def offer(chunk):
+        for index in range(chunk * size, (chunk + 1) * size):
+            comp = 0 if index == comps else index
+            mix = target_ref[...] if index == comps else mixer_ref[math.isqrt(comp)]
+            row = jnp.dot(pick, features_ref[comp], preferred_element_type=F32).astype(bf16)
+            outgoing[index] = jnp.dot(row, mix, preferred_element_type=F32).astype(bf16)
 
     pl.semaphore_wait(barrier, len(everyone))
-
-    size = (comps + 1) // CHUNKS
 
     def ship(chunk, source, slot, target, sem):
         rows = pl.ds(chunk * size, size)
@@ -344,58 +348,76 @@
                 device_id_type=MESH,
             ).start()
 
+    to_group(lambda i: about.at[me], lambda i: about.at[me], 0)
     for chunk in range(CHUNKS):
-        ship(chunk, own(chunk), 1, near["after"], near_recv.at[chunk, 0])
-        ship(chunk, own(chunk), 6, near["before"], near_recv.at[chunk, 0])
-        ship(chunk, own(chunk), 4 - core, near["outer"], near_recv.at[chunk, 1])
-        ship(chunk, own(chunk), 3 + core, near["pair"], halo_recv)
-        if chunk == 0:
-            to_group(lambda i: about.at[me], lambda i: about.at[me], 0)
+        offer(chunk)
+        ship(chunk, own(chunk), 0, near["after"], near_recv.at[chunk, 0])
+        ship(chunk, own(chunk), 1, near["before"], near_recv.at[chunk, 0])
+        ship(chunk, own(chunk), 3 - core, near["outer"], near_recv.at[chunk, 1])
+        ship(chunk, own(chunk), 2 + core, near["pair"], near_recv.at[chunk, 2])
+
+    def relay_outer(chunk):
+        all_of(got(chunk, 0), halo_send, near_recv.at[chunk, 1]).wait_recv()
+        ship(chunk, got(chunk, 2 + core), 4 + 3 * core, near["ahead"], halo_recv)
+
+    def relay_near(chunk):
+        both = arrived.at[pl.ds(chunk * size, size), pl.ds(0, 2)]
+        all_of(both, halo_send, near_recv.at[chunk, 0]).wait_recv()
+        ship(chunk, got(chunk, core), 5 + core, near["outer"], halo_recv)
+        ship(chunk, got(chunk, 0), 4 + core, near["pair"], halo_recv)
+        ship(chunk, got(chunk, 1), 6 + core, near["pair"], halo_recv)
+
+    def tables_of(first, stop):
+        fill_tables(first, stop, blocks, waves, about, sites, cos_ref, sin_ref)
 
     loads[7].wait()
     fill_mask(adjacency_ref, upright, mask_ref)
-    own_weights = attention(queries[...], table[comps], mask_ref[:, 0:LANES])
-    for comp in range(comps):
-        own_message[comp] = jnp.dot(own_weights, table[comp], preferred_element_type=F32)
-
+    relay_outer(0)
+    for degree, members in enumerate(degrees_of(comps)):
+        for comp in members:
+            product = jnp.dot(
+                features_ref[comp], mixer_ref[degree], preferred_element_type=F32
+            )
+            table[comp] = product.astype(bf16)
+    scalar = features_ref[0]
+    table[comps] = jnp.dot(scalar, target_ref[...], preferred_element_type=F32).astype(bf16)
+    queries[...] = jnp.dot(scalar, source_ref[...], preferred_element_type=F32).astype(bf16)
     for i in range(8, 11):
         loads[i].wait()
     others = about.at[pl.ds(0, group - 1)]
     all_of(others, group_send.at[0], group_recv.at[0]).wait_recv()
+    tables_of(0, group // 4)
+    relay_near(0)
+    relay_outer(1)
+    tables_of(group // 4, 3 * group // 4)
+    relay_near(1)
     for chunk in range(CHUNKS):
-        fill_tables(
-            chunk * group // CHUNKS,
-            (chunk + 1) * group // CHUNKS,
-            blocks,
-            waves,
-            about,
-            sites,
-            cos_ref,
-            sin_ref,
-        )
-        all_of(got(chunk, 0), halo_send, near_recv.at[chunk, 1]).wait_recv()
-        ship(chunk, got(chunk, 3 + core), 7 * core, near["ahead"], halo_recv)
-        both = arrived.at[pl.ds(chunk * size, size), pl.ds(0, 2)]
-        all_of(both, halo_send, near_recv.at[chunk, 0]).wait_recv()
-        ship(chunk, got(chunk, 1 + 5 * core), 2 + 3 * core, near["outer"], halo_recv)
-        ship(chunk, got(chunk, 1), 2 * core, near["pair"], halo_recv)
-        ship(chunk, got(chunk, 6), 5 + 2 * core, near["pair"], halo_recv)
+        all_of(got(chunk, 0), halo_send, near_recv.at[chunk, 2]).wait_recv()
+
+    def both_of(comp):
+        return jnp.concatenate([table[comp], arrived[comp, 0:4].reshape(4 * ghosts, LANES)], axis=0)
+
+    reach = LANES + 4 * ghosts
+    near_weights = attention(queries[...], both_of(comps), mask_ref[:, 0:reach])
+    for comp in range(comps):
+        own_message[comp] = jnp.dot(near_weights, both_of(comp), preferred_element_type=F32)
+    tables_of(3 * group // 4, group)
     for member in range(group):
         vectors[3, member : member + 1, :] = about[member, 3:4, :]
         vectors[4, member : member + 1, :] = about[member, 4:5, :]
     vectors[1] = jnp.zeros((group, LANES), F32)
     vectors[2] = jnp.zeros((group, LANES), F32)
     factors[...] = jnp.zeros_like(factors)
-    all_of(arrived.at[:, pl.ds(0, 5)], halo_send, halo_recv).wait_recv()
-
-    ghost_keys = arrived[comps].reshape(8 * ghosts, LANES)
-    weights = attention(queries[...], ghost_keys, mask_ref[:, LANES:])
+    all_of(arrived.at[:, pl.ds(0, 4)], halo_send, halo_recv).wait_recv()
+
+    far_keys = arrived[comps, 4:8].reshape(4 * ghosts, LANES)
+    weights = attention(queries[...], far_keys, mask_ref[:, reach:])
     readout = jnp.zeros((LANES, LANES), F32)
     for degree, members in enumerate(degrees_of(comps)):
         square = jnp.zeros((LANES, LANES), F32)
         for comp in members:
             message = own_message[comp] + jnp.dot(
-                weights, arrived[comp].reshape(8 * ghosts, LANES), preferred_element_type=F32
+                weights, arrived[comp, 4:8].reshape(4 * ghosts, LANES), preferred_element_type=F32
             )
             square = message if degree == 0 else square + message * message
         norm = square if degree == 0 else jnp.sqrt(square + 1e-06)
@@ -403,10 +425,8 @@
     electroneg = row_of(jnp.sum(readout, axis=1, keepdims=True), eye) + baseline
     first_rows[me] = -electroneg * live
     to_group(lambda i: first_rows.at[me], lambda i: first_rows.at[me], 1)
-    all_of(arrived, halo_send, halo_recv).wait_send()
-    all_of(others, group_send.at[0], group_recv.at[0]).wait_send()
     starts = first_rows.at[pl.ds(0, group - 1)]
-    all_of(starts, group_send.at[1], group_recv.at[1]).wait()
+    all_of(starts, group_send.at[1], group_recv.at[1]).wait_recv()
     for member in range(group):
         vectors[0, member : member + 1, :] = first_rows[member]
 
@@ -441,6 +461,13 @@
             row = scalar_row + i
             parts[turn, 0, row : row + 1, :] = jnp.broadcast_to(full_sum(product), (1, LANES))
 
+    def ring_stage(turn, stage):
+        sems = (ring_send.at[turn, stage], ring_recv.at[turn, stage])
+        return all_of(inbox.at[turn, stage], *sems)
+
+    def post_stage(turn):
+        return all_of(post_inbox.at[turn], group_send.at[2 + turn], group_recv.at[2 + turn])
+
     def ring_sum(turn, meanwhile):
         held = parts[turn, 0]
         for stage, targets in enumerate((along, across)):
@@ -450,14 +477,14 @@
                 pltpu.make_async_remote_copy(
                     src_ref=parts.at[turn, stage],
                     dst_ref=inbox.at[turn, stage, i],
-                    send_sem=ring_send.at[stage],
+                    send_sem=ring_send.at[turn, stage],
                     recv_sem=ring_recv.at[turn, stage],
                     device_id=target,
                     device_id_type=MESH,
                 ).start()
             if stage == 0:
                 meanwhile()
-            all_of(inbox.at[turn, stage], ring_send.at[stage], ring_recv.at[turn, stage]).wait()
+            ring_stage(turn, stage).wait_recv()
             for i in range(len(targets)):
                 held = held + inbox[turn, stage, i]
         ring_total[...] = held
@@ -482,20 +509,23 @@
         ring_sum(turn, lambda: None)
         norm, stiff_part, recip = follow(turn, *carry)
 
-        def back(member, acc):
-            image = jnp.zeros((LANES, LANES), F32)
-            for block in range(blocks):
-                for part in range(2):
-                    row = factors[2 + part, block : block + 1, :]
-                    image = image + tables[part][member * blocks + block] * row
-            return jnp.where(lanes == member, jnp.sum(image, axis=1, keepdims=True), acc)
-
-        images = lax.fori_loop(0, group, back, jnp.zeros((LANES, LANES), F32))
+        def back(step, acc):
+            for j in range(2):
+                member = 2 * step + j
+                image = jnp.zeros((LANES, LANES), F32)
+                for block in range(blocks):
+                    for part in range(2):
+                        row = factors[2 + part, block : block + 1, :]
+                        image = image + tables[part][member * blocks + block] * row
+                acc = jnp.where(lanes == member, jnp.sum(image, axis=1, keepdims=True), acc)
+            return acc
+
+        images = lax.fori_loop(0, group // 2, back, jnp.zeros((LANES, LANES), F32))
         posts[turn, 0:group, :] = images.T[0:group, :]
         posts[turn, group : group + 1, :] = recip
         to_group(lambda i: posts.at[turn], lambda i: post_inbox.at[turn, i], 2 + turn)
         held = posts[turn]
-        all_of(post_inbox.at[turn], group_send.at[2 + turn], group_recv.at[2 + turn]).wait()
+        post_stage(turn).wait_recv()
         for i in range(group - 1):
             held = held + post_inbox[turn, i]
         post_total[...] = held
@@ -511,9 +541,10 @@
     def field_of(first, offset):
         half = LANES // 2
 
-        def per_member(member, carry):
-            for part in range(2):
-                rows = pl.ds(part * half, half)
+        def per_pair(step, carry):
+            for part in range(4):
+                member = 2 * step + part // 2
+                rows = pl.ds(part % 2 * half, half)
                 sums = [jnp.zeros((half, LANES), F32) for _ in range(3)]
                 for block in range(blocks):
                     where = member * blocks + block
@@ -532,7 +563,7 @@
                 matrix[rows, :] = filled
             return carry
 
-        lax.fori_loop(0, group, per_member, 0)
+        lax.fori_loop(0, group // 2, per_pair, 0)
 
     ones = jnp.ones((1, LANES), F32)
     carry = lax.fori_loop(0, ITERS - 1, iteration, (ones, ones))
@@ -550,6 +581,14 @@
     stage = 1 + ITERS
     to_group(lambda i: fields.at[peers[i][0]], lambda i: field_inbox.at[i], stage)
     held = fields[me]
+    all_of(arrived, halo_send, halo_recv).wait_send()
+    all_of(others, group_send.at[0], group_recv.at[0]).wait_send()
+    all_of(starts, group_send.at[1], group_recv.at[1]).wait_send()
+    for sent in range(ITERS):
+        ring_stage(sent, 0).wait_send()
+        ring_stage(sent, 1).wait_send()
+        if sent < turn:
+            post_stage(sent).wait_send()
     all_of(field_inbox, group_send.at[stage], group_recv.at[stage]).wait()
     for i in range(group - 1):
         held = held + field_inbox[i]
@@ -587,6 +626,7 @@
     ghosts = halo_export_indices.shape[2]
     degrees = degree_channel_mixer.shape[0]
     lists = adjacency_rows.shape[3]
+    elements = chemical_stiffness.shape[0]
     group = 2 * chips_x
     blocks = reciprocal_lattice_points.shape[1] // LANES // group
     rows = 2 * blocks + SCALARS
@@ -597,6 +637,21 @@
     smem = pl.BlockSpec(memory_space=pltpu.SMEM)
     hbm = pl.BlockSpec(memory_space=pltpu.HBM)
     dma = pltpu.SemaphoreType.DMA
+    operands = (
+        jnp.transpose(equivariant_embedding[0, 0], (1, 0, 2)),
+        degree_channel_mixer,
+        attention_source_weights,
+        attention_target_weights,
+        halo_export_indices[0],
+        cartesian_coordinates[0, 0].reshape(3, 1, LANES),
+        element_identity[0],
+        adjacency_rows[0, 0].T,
+        affinity_output_head,
+        ewald_weighting.reshape(group, blocks, LANES),
+        reciprocal_lattice_points,
+        baseline_affinity_per_element.reshape(1, elements),
+        chemical_stiffness.reshape(1, elements),
+    )
     charges, forces = pl.pallas_call(
         lambda *refs: whole_kernel(shape, *refs),
         name="equilibrate",
@@ -604,7 +659,7 @@
             jax.ShapeDtypeStruct((1, LANES), F32),
             jax.ShapeDtypeStruct((3, 1, LANES), F32),
         ),
-        in_specs=[hbm] * 11 + [smem] * 3,
+        in_specs=[hbm] * 13 + [smem],
         out_specs=(vmem, vmem),
         scratch_shapes=[
             pltpu.VMEM((comps, LANES, LANES), bf16),
@@ -618,6 +673,8 @@
             pltpu.VMEM((degrees, LANES), F32),
             pltpu.VMEM((group, blocks, LANES), F32),
             pltpu.VMEM((3, blocks * LANES), F32),
+            pltpu.VMEM((1, elements), F32),
+            pltpu.VMEM((1, elements), F32),
             pltpu.VMEM((LANES, LANES), bf16),
             pltpu.VMEM((comps + 1, LANES, LANES), bf16),
             pltpu.VMEM((comps + 1, ghosts, LANES), bf16),
@@ -641,34 +698,19 @@
             pltpu.VMEM((LANES, LANES), F32),
             pltpu.VMEM((group, TILE, LANES), F32),
             pltpu.VMEM((group - 1, TILE, LANES), F32),
-            dma((11,)),
+            dma((13,)),
             dma,
             dma,
-            dma((CHUNKS, 2)),
+            dma((CHUNKS, 3)),
             dma((ITERS + 2,)),
             dma((ITERS + 2,)),
-            dma((2,)),
+            dma((ITERS, 2)),
             dma((ITERS, 2)),
         ],
         compiler_params=pltpu.CompilerParams(
             collective_id=1, has_side_effects=True, vmem_limit_bytes=48 * 1024 * 1024
         ),
-    )(
-        jnp.transpose(equivariant_embedding[0, 0], (1, 0, 2)),
-        degree_channel_mixer,
-        attention_source_weights,
-        attention_target_weights,
-        halo_export_indices[0],
-        cartesian_coordinates[0, 0].reshape(3, 1, LANES),
-        element_identity[0],
-        adjacency_rows[0, 0].T,
-        affinity_output_head,
-        ewald_weighting.reshape(group, blocks, LANES),
-        reciprocal_lattice_points,
-        occupied_site_totals,
-        baseline_affinity_per_element,
-        chemical_stiffness,
-    )
+    )(*(pltpu.with_memory_space_constraint(item, pltpu.HBM) for item in operands), occupied_site_totals)
     return (charges.reshape(1, 1, LANES), forces.reshape(1, 1, 3, LANES))
 
 

time: 104 us -> 94.1 us (0.905)
  local copies, waits for them, and re-layouts: 7.65 us -> 1.07 us
  Pallas kernels: 94.6 us -> 91.6 us
    unnamed x28 -> x2, local copies, waits for them, and re-layouts: 7.65 us -> 1.07 us
    pallas_call x1, Pallas kernels: 94.6 us -> 91.6 us  [shards(): pl.pallas_call(lambda *refs: whole_kernel(shape, *refs), name='equilibrat...]
where the time goes in v4:
time: 94.1 us; the launch traced here: 93.9 us
  Pallas kernels  91.6 us (97%)
  between operations  1.29 us (1%)
  local copies, waits for them, and re-layouts  1.07 us (1%)
    pallas_call x1, Pallas kernels, shards(): pl.pallas_call(lambda *refs: whole_kernel(shape, *refs), name='equilibrat...  91.6 us

profile of v4, /device:TPU:1, one launch (start us, length us, event | category | flops | bytes accessed | tf_op | source)
XLA Modules:
  0.0 93.9 jit_solution(7730716937229802719)
XLA Ops:
  1.3 91.6 %equilibrate.1 = (f32[1,128]{1,0:T(1,128)S(1)}, f32[3,1,128]{2,1,0:T(1,128)S(1)}) custom-call(bf16[25,128,128]{2,1,0:T(8,128)(2,1)} %bitcast.18, bf16[5,128,128]{2,1,0:T(8,128)(2,1)} %refs_1_.1, bf16[128,128]{1,0:T(8,128)(2,1)} %refs_2_.1, bf16[128,128]{1,0:T(8,128)(2,1)} %refs_3_.1, s32[1,32]{1,0:T(1,128)} %bitcast.22, f32[3,1,128]{2,1,0:T(1,128)} %bitcast.21, ...), custom_call_target="tpu_custom_call" | custom-call | tf_op jit(solution)/shard_map/equilibrate/pallas_call | solution.py:655
  92.8 0.5 copy.20
  93.4 0.6 copy.21

commit v5 on v4

--- a/solution.py
+++ b/solution.py
@@ -35,7 +35,7 @@
     return sine, cosine
 
 
-CHUNKS = 2
+CHUNKS = ((0, 13), (13, 8), (21, 5))
 BLOCKS = (1, 7, 3, 5, 0, 2, 6, 8)
 SCALARS = 3
 TILE = 8
@@ -58,12 +58,12 @@
 def sum_partners(shape):
     x, y, z, core = place_of(shape)
     chips_x, ring, _ = shape
-    group = 2 * chips_x
     mine = x * 2 + core
     peers = []
-    for i in far_first(group):
-        other = lax.rem(mine + i, group)
-        peers.append((other, device(shape, lax.div(other, 2), y, z, lax.rem(other, 2))))
+    steps = [(dx, dc) for dx in far_first(chips_x) for dc in (0, 1)] + [(0, 1)]
+    for dx, dc in steps:
+        other_x, other_core = lax.rem(x + dx, chips_x), lax.rem(core + dc, 2)
+        peers.append((other_x * 2 + other_core, device(shape, other_x, y, z, other_core)))
     along = [
         device(shape, x, lax.rem(y + j * (1 - core), ring), lax.rem(z + j * core, ring), core)
         for j in far_first(ring)
@@ -298,10 +298,8 @@
     offered = jnp.sum(jnp.where(identity_mask(ghosts), offered, 0.0), axis=1, keepdims=True)
     slots = lax.broadcasted_iota(jnp.int32, (ghosts, LANES), 1).astype(F32)
     pick = jnp.where(slots == offered, 1.0, 0.0).astype(bf16)
-    size = (comps + 1) // CHUNKS
-
     def offer(chunk):
-        for index in range(chunk * size, (chunk + 1) * size):
+        for index in range(CHUNKS[chunk][0], sum(CHUNKS[chunk])):
             comp = 0 if index == comps else index
             mix = target_ref[...] if index == comps else mixer_ref[math.isqrt(comp)]
             row = jnp.dot(pick, features_ref[comp], preferred_element_type=F32).astype(bf16)
@@ -310,7 +308,7 @@
     pl.semaphore_wait(barrier, len(everyone))
 
     def ship(chunk, source, slot, target, sem):
-        rows = pl.ds(chunk * size, size)
+        rows = pl.ds(*CHUNKS[chunk])
         copy = pltpu.make_async_remote_copy(
             src_ref=source,
             dst_ref=arrived.at[rows, slot],
@@ -322,10 +320,10 @@
         copy.start()
 
     def own(chunk):
-        return outgoing.at[pl.ds(chunk * size, size)]
+        return outgoing.at[pl.ds(*CHUNKS[chunk])]
 
     def got(chunk, slot):
-        return arrived.at[pl.ds(chunk * size, size), slot]
+        return arrived.at[pl.ds(*CHUNKS[chunk]), slot]
 
     def all_of(ref, send, receive):
         return pltpu.make_async_remote_copy(
@@ -349,7 +347,7 @@
             ).start()
 
     to_group(lambda i: about.at[me], lambda i: about.at[me], 0)
-    for chunk in range(CHUNKS):
+    for chunk in range(len(CHUNKS)):
         offer(chunk)
         ship(chunk, own(chunk), 0, near["after"], near_recv.at[chunk, 0])
         ship(chunk, own(chunk), 1, near["before"], near_recv.at[chunk, 0])
@@ -361,7 +359,7 @@
         ship(chunk, got(chunk, 2 + core), 4 + 3 * core, near["ahead"], halo_recv)
 
     def relay_near(chunk):
-        both = arrived.at[pl.ds(chunk * size, size), pl.ds(0, 2)]
+        both = arrived.at[pl.ds(*CHUNKS[chunk]), pl.ds(0, 2)]
         all_of(both, halo_send, near_recv.at[chunk, 0]).wait_recv()
         ship(chunk, got(chunk, core), 5 + core, near["outer"], halo_recv)
         ship(chunk, got(chunk, 0), 4 + core, near["pair"], halo_recv)
@@ -389,9 +387,12 @@
     tables_of(0, group // 4)
     relay_near(0)
     relay_outer(1)
-    tables_of(group // 4, 3 * group // 4)
+    tables_of(group // 4, group // 2)
     relay_near(1)
-    for chunk in range(CHUNKS):
+    relay_outer(2)
+    tables_of(group // 2, 5 * group // 8)
+    relay_near(2)
+    for chunk in range(len(CHUNKS)):
         all_of(got(chunk, 0), halo_send, near_recv.at[chunk, 2]).wait_recv()
 
     def both_of(comp):
@@ -401,7 +402,7 @@
     near_weights = attention(queries[...], both_of(comps), mask_ref[:, 0:reach])
     for comp in range(comps):
         own_message[comp] = jnp.dot(near_weights, both_of(comp), preferred_element_type=F32)
-    tables_of(3 * group // 4, group)
+    tables_of(5 * group // 8, group)
     for member in range(group):
         vectors[3, member : member + 1, :] = about[member, 3:4, :]
         vectors[4, member : member + 1, :] = about[member, 4:5, :]
@@ -457,9 +458,10 @@
                 )
         hard_residual = vectors[3] * residual
         scalars = (residual * residual, hard_residual * residual, hard_residual * vectors[1])
+        row = jnp.zeros((1, LANES), F32)
         for i, product in enumerate(scalars):
-            row = scalar_row + i
-            parts[turn, 0, row : row + 1, :] = jnp.broadcast_to(full_sum(product), (1, LANES))
+            row = jnp.where(lanes[0:1, :] == i, full_sum(product), row)
+        parts[turn, 0, scalar_row : scalar_row + 1, :] = row
 
     def ring_stage(turn, stage):
         sems = (ring_send.at[turn, stage], ring_recv.at[turn, stage])
@@ -491,7 +493,8 @@
 
     def follow(turn, previous_norm, stiff_part):
         norm, pure, mixed = (
-            ring_total[scalar_row + i : scalar_row + i + 1, :] for i in range(SCALARS)
+            jnp.broadcast_to(ring_total[scalar_row : scalar_row + 1, i : i + 1], (1, LANES))
+            for i in range(SCALARS)
         )
         beta = jnp.where(turn > 0, norm / previous_norm, 0.0)
         stiff_part = pure + 2.0 * beta * mixed + beta * beta * stiff_part
@@ -629,10 +632,10 @@
     elements = chemical_stiffness.shape[0]
     group = 2 * chips_x
     blocks = reciprocal_lattice_points.shape[1] // LANES // group
-    rows = 2 * blocks + SCALARS
+    rows = 2 * blocks + 1
     table_size = LANES + 8 * ghosts
     bf16, i32 = jnp.bfloat16, jnp.int32
-    assert group * TILE <= LANES and (comps + 1) % CHUNKS == 0
+    assert group * TILE <= LANES and comps + 1 == sum(CHUNKS[-1])
     vmem = pl.BlockSpec(memory_space=pltpu.VMEM)
     smem = pl.BlockSpec(memory_space=pltpu.SMEM)
     hbm = pl.BlockSpec(memory_space=pltpu.HBM)
@@ -701,7 +704,7 @@
             dma((13,)),
             dma,
             dma,
-            dma((CHUNKS, 3)),
+            dma((len(CHUNKS), 3)),
             dma((ITERS + 2,)),
             dma((ITERS + 2,)),
             dma((ITERS, 2)),

time: 94.1 us -> 92.4 us (0.982)
  Pallas kernels: 91.6 us -> 89.9 us
    pallas_call x1, Pallas kernels: 91.6 us -> 89.9 us  [shards(): pl.pallas_call(lambda *refs: whole_kernel(shape, *refs), name='equilibrat...]
where the time goes in v5:
time: 92.4 us; the launch traced here: 92.3 us
  Pallas kernels  89.9 us (97%)
  between operations  1.29 us (1%)
  local copies, waits for them, and re-layouts  1.07 us (1%)
    pallas_call x1, Pallas kernels, shards(): pl.pallas_call(lambda *refs: whole_kernel(shape, *refs), name='equilibrat...  89.9 us

profile of v5, /device:TPU:1, one launch (start us, length us, event | category | flops | bytes accessed | tf_op | source)
XLA Modules:
  0.0 92.3 jit_solution(12780230363821729596)
XLA Ops:
  1.3 89.9 %equilibrate.1 = (f32[1,128]{1,0:T(1,128)S(1)}, f32[3,1,128]{2,1,0:T(1,128)S(1)}) custom-call(bf16[25,128,128]{2,1,0:T(8,128)(2,1)} %bitcast.18, bf16[5,128,128]{2,1,0:T(8,128)(2,1)} %refs_1_.1, bf16[128,128]{1,0:T(8,128)(2,1)} %refs_2_.1, bf16[128,128]{1,0:T(8,128)(2,1)} %refs_3_.1, s32[1,32]{1,0:T(1,128)} %bitcast.22, f32[3,1,128]{2,1,0:T(1,128)} %bitcast.21, ...), custom_call_target="tpu_custom_call" | custom-call | tf_op jit(solution)/shard_map/equilibrate/pallas_call | solution.py:658
  91.2 0.5 copy.20
  91.7 0.6 copy.21

commit v6 on v5

--- a/solution.py
+++ b/solution.py
@@ -13,14 +13,13 @@
 MESH = pl.DeviceIdType.MESH
 F32 = jnp.float32
 
-HALF_PI_PARTS = (1.5703125, 4.837512969970703125e-4, 7.54978995489188216e-8)
+HALF_PI_PARTS = (1.57080078125, math.pi / 2 - 1.57080078125)
 
 
 def sine_cosine(phase):
     quadrant = jnp.round(phase * (2.0 / math.pi))
     reduced = phase - quadrant * HALF_PI_PARTS[0]
     reduced = reduced - quadrant * HALF_PI_PARTS[1]
-    reduced = reduced - quadrant * HALF_PI_PARTS[2]
     square = reduced * reduced
     odd = (-1.9515295891e-4 * square + 8.3321608736e-3) * square - 1.6666654611e-1
     odd = odd * square * reduced + reduced
@@ -513,8 +512,8 @@
         norm, stiff_part, recip = follow(turn, *carry)
 
         def back(step, acc):
-            for j in range(2):
-                member = 2 * step + j
+            for j in range(4):
+                member = 4 * step + j
                 image = jnp.zeros((LANES, LANES), F32)
                 for block in range(blocks):
                     for part in range(2):
@@ -523,7 +522,7 @@
                 acc = jnp.where(lanes == member, jnp.sum(image, axis=1, keepdims=True), acc)
             return acc
 
-        images = lax.fori_loop(0, group // 2, back, jnp.zeros((LANES, LANES), F32))
+        images = lax.fori_loop(0, group // 4, back, jnp.zeros((LANES, LANES), F32))
         posts[turn, 0:group, :] = images.T[0:group, :]
         posts[turn, group : group + 1, :] = recip
         to_group(lambda i: posts.at[turn], lambda i: post_inbox.at[turn, i], 2 + turn)
@@ -603,6 +602,11 @@
     for axis in range(3):
         field = fields[me, axis : axis + 1, :] + step * fields[me, 3 + axis : 4 + axis, :]
         forces_ref[axis] = charges * (scale * field)
+
+
+def hand_over(charges_ref, forces_ref, charges_out, forces_out):
+    charges_out[...] = charges_ref[...]
+    forces_out[...] = forces_ref[...]
 
 
 def shards(
@@ -714,6 +718,17 @@
             collective_id=1, has_side_effects=True, vmem_limit_bytes=48 * 1024 * 1024
         ),
     )(*(pltpu.with_memory_space_constraint(item, pltpu.HBM) for item in operands), occupied_site_totals)
+    charges, forces = pl.pallas_call(
+        hand_over,
+        name="results",
+        out_shape=(
+            jax.ShapeDtypeStruct((1, LANES), F32),
+            jax.ShapeDtypeStruct((3, 1, LANES), F32),
+        ),
+        in_specs=[vmem, vmem],
+        out_specs=(vmem, vmem),
+        compiler_params=pltpu.CompilerParams(vmem_limit_bytes=1024 * 1024),
+    )(charges, forces)
     return (charges.reshape(1, 1, LANES), forces.reshape(1, 1, 3, LANES))
 
 

time: 92.4 us -> 91.4 us (0.989)
  local copies, waits for them, and re-layouts: 1.07 us -> 0 us
    unnamed x2 -> x0, local copies, waits for them, and re-layouts: 1.07 us -> none
where the time goes in v6:
time: 91.4 us; the launch traced here: 91.3 us
  Pallas kernels  90 us (98%)
  between operations  1.29 us (1%)
    pallas_call x1, Pallas kernels, shards(): pl.pallas_call(lambda *refs: whole_kernel(shape, *refs), name='equilibrat...  89.4 us

profile of v6, /device:TPU:1, one launch (start us, length us, event | category | flops | bytes accessed | tf_op | source)
XLA Modules:
  0.0 91.3 jit_solution(534417501525919852)
XLA Ops:
  1.3 89.4 %equilibrate.1 = (f32[1,128]{1,0:T(1,128)S(1)}, f32[3,1,128]{2,1,0:T(1,128)S(1)}) custom-call(bf16[25,128,128]{2,1,0:T(8,128)(2,1)} %bitcast.16, bf16[5,128,128]{2,1,0:T(8,128)(2,1)} %refs_1_.1, bf16[128,128]{1,0:T(8,128)(2,1)} %refs_2_.1, bf16[128,128]{1,0:T(8,128)(2,1)} %refs_3_.1, s32[1,32]{1,0:T(1,128)} %bitcast.20, f32[3,1,128]{2,1,0:T(1,128)} %bitcast.19, ...), custom_call_target="tpu_custom_call" | custom-call | tf_op jit(solution)/shard_map/equilibrate/pallas_call | solution.py:662
  90.7 0.6 results.1
